TPU v7x, 128 devices: a whole 4x4x4 slice. The times are simulated.
128 devices in a mesh: req: 8 (over x, core), mlp: 16 (over y, z).
Axes of the slice: x: 4, y: 4, z: 4, core: 2. Of those that a mesh axis runs over, the one named last changes fastest.
Arguments:
- queries: bfloat16 [4096, 4096], P(('req', 'mlp')), may hold values from -80 to 80
- keys: bfloat16 [4096, 4096], P(('req', 'mlp')), may hold values from -4 to 4
- values: bfloat16 [4096, 4096], P(('req', 'mlp')), may hold values from -6 to 6
- block_hidden_input: bfloat16 [4096, 5120], P(('req', 'mlp')), may hold values from -6 to 6
- attention_out_weight: bfloat16 [4096, 5120], P('mlp'), may hold values from -0.09375 to 0.09375
- feedfwd_in_weight: bfloat16 [5120, 13824], P(None, 'mlp'), may hold values from -0.078125 to 0.078125
- feedfwd_out_weight: bfloat16 [13824, 5120], P('mlp'), may hold values from -0.0546875 to 0.0546875
- norm_gain_vector: float32 [5120], replicated, may hold values from 0.5 to 1.5
- norm_bias_vector: float32 [5120], replicated, may hold values from -3 to 3
- adapter_down_factors: bfloat16 [64, 5120, 16], P('req', 'mlp'), may hold values from -0.078125 to 0.078125
- adapter_up_factors: bfloat16 [64, 16, 13824], P('req', None, 'mlp'), may hold values from -0.75 to 0.75
- paged_key_cache: bfloat16 [40, 128, 4096], P('req', None, 'mlp'), may hold values from -6 to 6
- paged_value_cache: bfloat16 [40, 128, 4096], P('req', None, 'mlp'), may hold values from -6 to 6
- request_prompt_length: int32 [8, 16], P('req'), may hold values from 1 to 256, 512 in all within a row
- group_page_lookup: int32 [8, 4], P('req'), may hold values from 0 to 4, as said below
- adapter_per_request: int32 [8, 16], P('req'), may hold values from 0 to 63
- adapter_bank_slot: int32 [64], replicated, may hold values from 0 to 63, each once
Outputs:
- block_out: bfloat16 [4096, 5120], P(('req', 'mlp'))
- key_pages_out: bfloat16 [40, 128, 4096], P('req', None, 'mlp')
- value_pages_out: bfloat16 [40, 128, 4096], P('req', None, 'mlp')
Inputs may be any that keep to these rules, and one draw needn't show every extreme that they name: `group_page_lookup`: the 4 entries of a row are different pages of the group's 5. `request_prompt_length`: each row sums to 512; its longest request holds exactly half of that.
All inputs are finite; a program needn't handle non-finite values.
Results may differ from a plain program's by a relative error of at most 0.014.
Values may be sent and summed in bfloat16 or wider, within the bound.
A program may use at most 128 MiB of HBM per device.

v0:
```python
import jax
import jax.numpy as jnp
from jax import lax
from jax.sharding import PartitionSpec as P

HS = 128
ADAPTER_RANK = 16
REQS = 16
PAGE = 128


EPS = 1e-06


def modulate(residual, norm_gain_vector, norm_bias_vector):
    row_mean = jnp.mean(residual, axis=-1, keepdims=True)
    centered = residual - row_mean
    row_var = jnp.mean(centered * centered, axis=-1, keepdims=True)
    return (centered * lax.rsqrt(row_var + EPS) * norm_gain_vector + norm_bias_vector).astype(
        jnp.bfloat16
    )


def softmax_rows(scores, allowed):
    masked = jnp.where(allowed, scores, -1e30)
    row_peak = jnp.max(masked, axis=-1, keepdims=True)
    exponent = jnp.exp(masked - row_peak)
    return (exponent / jnp.sum(exponent, axis=-1, keepdims=True)).astype(jnp.bfloat16)


def shards(
    queries,
    keys,
    values,
    block_hidden_input,
    attention_out_weight,
    feedfwd_in_weight,
    feedfwd_out_weight,
    norm_gain_vector,
    norm_bias_vector,
    adapter_down_factors,
    adapter_up_factors,
    paged_key_cache,
    paged_value_cache,
    request_prompt_length,
    group_page_lookup,
    adapter_per_request,
    adapter_bank_slot,
):
    tok_rows = block_hidden_input.shape[0]
    groups = lax.axis_size("mlp")
    group_rows = tok_rows * groups
    head_cols = attention_out_weight.shape[0]
    local_heads = head_cols // HS
    column_index = lax.axis_index("mlp")
    query_all, key_all, value_all = (
        lax.all_to_all(queries, "mlp", split_axis=1, concat_axis=0, tiled=True),
        lax.all_to_all(keys, "mlp", split_axis=1, concat_axis=0, tiled=True),
        lax.all_to_all(values, "mlp", split_axis=1, concat_axis=0, tiled=True),
    )
    adapter_ids = adapter_per_request[0]
    matched = (
        adapter_ids[:, None] == jnp.arange(adapter_bank_slot.shape[0], dtype=jnp.int32)[None, :]
    )
    wanted = jnp.sum(jnp.where(matched, adapter_bank_slot[None, :], 0), axis=1)
    down_factor_piece = lax.all_gather(adapter_down_factors, "req", axis=0, tiled=True)
    up_factor_piece = lax.all_gather(adapter_up_factors, "req", axis=0, tiled=True)
    row_count = down_factor_piece.shape[0]
    onehot = (wanted[:, None] == jnp.arange(row_count, dtype=jnp.int32)[None, :]).astype(
        jnp.bfloat16
    )
    down_add = jnp.einsum(
        "rn,ndk->rdk", onehot, down_factor_piece, preferred_element_type=jnp.float32
    )
    up_add = jnp.einsum("rn,nkf->rkf", onehot, up_factor_piece, preferred_element_type=jnp.float32)
    down_factor_chosen = down_add
    up_factor_chosen = up_add
    down_factor_chosen = down_factor_chosen.astype(jnp.bfloat16)
    up_factor_chosen = up_factor_chosen.astype(jnp.bfloat16)
    request_ends = jnp.cumsum(request_prompt_length[0])
    positions = jnp.arange(group_rows, dtype=jnp.int32)
    segment = jnp.sum((positions[:, None] >= request_ends[None, :]).astype(jnp.int32), axis=1)
    chosen = segment[:, None] == jnp.arange(REQS, dtype=jnp.int32)[None, :]
    query_heads = query_all.reshape(group_rows, local_heads, HS)
    key_heads = key_all.reshape(group_rows, local_heads, HS)
    value_heads = value_all.reshape(group_rows, local_heads, HS)
    score_scale = HS ** (-0.5)
    block_rows = min(512, group_rows)
    scores = (
        jnp.einsum("qhd,khd->hqk", query_heads, key_heads, preferred_element_type=jnp.float32)
        * score_scale
    )
    allowed = (segment[:, None] == segment[None, :]) & (positions[None, :] <= positions[:, None])
    weights = softmax_rows(scores, allowed[None])
    mixed = jnp.einsum("hqk,khd->qhd", weights, value_heads, preferred_element_type=jnp.float32)
    pieces_out = mixed.astype(jnp.bfloat16).reshape(block_rows, head_cols)
    page_count = group_rows // PAGE
    key_pages_out = paged_key_cache.at[group_page_lookup[0]].set(
        key_all.reshape(page_count, PAGE, head_cols)
    )
    value_pages_out = paged_value_cache.at[group_page_lookup[0]].set(
        value_all.reshape(page_count, PAGE, head_cols)
    )
    row_block = pieces_out
    residual = block_hidden_input.astype(jnp.float32) + lax.psum_scatter(
        jnp.dot(row_block, attention_out_weight, preferred_element_type=jnp.float32).astype(
            jnp.bfloat16
        ),
        "mlp",
        scatter_dimension=0,
        tiled=True,
    ).astype(jnp.float32)
    normed_all = lax.all_gather(
        modulate(residual, norm_gain_vector, norm_bias_vector), "mlp", axis=0, tiled=True
    )
    width_dev = down_factor_chosen.shape[1]
    column_block = lax.dynamic_slice_in_dim(normed_all, column_index * width_dev, width_dev, 1)
    down_flat = jnp.transpose(down_factor_chosen, (1, 0, 2)).reshape(width_dev, REQS * ADAPTER_RANK)
    every_rank = jnp.dot(column_block, down_flat, preferred_element_type=jnp.float32).reshape(
        group_rows, REQS, ADAPTER_RANK
    )
    own_rank = jnp.sum(every_rank * chosen.astype(jnp.float32)[:, :, None], axis=1)
    lowrank = lax.psum(own_rank.astype(jnp.bfloat16), "mlp")
    spread = (chosen.astype(jnp.bfloat16)[:, :, None] * lowrank[:, None, :]).reshape(
        group_rows, REQS * ADAPTER_RANK
    )
    up_flat = up_factor_chosen.reshape(REQS * ADAPTER_RANK, up_factor_chosen.shape[2])
    preact = jnp.dot(normed_all, feedfwd_in_weight, preferred_element_type=jnp.float32) + jnp.dot(
        spread, up_flat, preferred_element_type=jnp.float32
    )
    activated = jax.nn.gelu(preact, approximate=True).astype(jnp.bfloat16)
    row_block = activated
    mlp_out = lax.psum_scatter(
        jnp.dot(row_block, feedfwd_out_weight, preferred_element_type=jnp.float32).astype(
            jnp.bfloat16
        ),
        "mlp",
        scatter_dimension=0,
        tiled=True,
    ).astype(jnp.float32)
    block_out = (residual + mlp_out).astype(jnp.bfloat16)
    return (block_out, key_pages_out, value_pages_out)


def solution(mesh):
    in_specs = (
        P(("req", "mlp"), None),
        P(("req", "mlp"), None),
        P(("req", "mlp"), None),
        P(("req", "mlp"), None),
        P("mlp", None),
        P(None, "mlp"),
        P("mlp", None),
        P(),
        P(),
        P("req", "mlp", None),
        P("req", None, "mlp"),
        P("req", None, "mlp"),
        P("req", None, "mlp"),
        P("req", None),
        P("req", None),
        P("req", None),
        P(),
    )
    out_specs = (P(("req", "mlp"), None), P("req", None, "mlp"), P("req", None, "mlp"))
    return jax.shard_map(shards, mesh=mesh, in_specs=in_specs, out_specs=out_specs, check_vma=False)
```

profile of v0, /device:TPU:0, one launch (start us, length us, event | category | flops | bytes accessed | tf_op | source)
XLA Modules:
  0.0 383.9 jit_solution(17641889858919498241)
XLA Ops:
  8.0 1.9 copy.113
  9.9 1.7 copy.114
  11.6 1.7 copy.106
  13.3 8.2 %all-to-all-start.1 = ((bf16[32,16,256]{2,0,1:T(8,128)(2,1)}), bf16[32,16,256]{2,0,1:T(8,128)(2,1)S(1)}, u32[]{:S(2)}, u32[]{:S(2)}) async-start(bf16[32,16,256]{2,0,1:T(8,128)(2,1)} %bitcast.53), calls=%async_computation.1 | async-start | bytes 524288 | tf_op jit(solution)/shard_map/all_to_all | solution.py:58
  22.2 7.8 %all-to-all-done.1 = bf16[32,16,256]{2,0,1:T(8,128)(2,1)S(1)} async-done(((bf16[32,16,256]{2,0,1:T(8,128)(2,1)}), bf16[32,16,256]{2,0,1:T(8,128)(2,1)S(1)}, u32[]{:S(2)}, u32[]{:S(2)}) %all-to-all-start.1) | async-done | bytes 262176 | tf_op jit(solution)/shard_map/all_to_all | solution.py:58
  30.0 3.6 all-to-all-start
  35.5 6.5 %all-to-all-done = bf16[32,16,256]{2,0,1:T(8,128)(2,1)S(1)} async-done(((bf16[32,16,256]{2,0,1:T(8,128)(2,1)}), bf16[32,16,256]{2,0,1:T(8,128)(2,1)S(1)}, u32[]{:S(2)}, u32[]{:S(2)}) %all-to-all-start) | async-done | bytes 262176 | tf_op jit(solution)/shard_map/all_to_all | solution.py:57
  42.1 3.7 all-to-all-start.2
  48.4 5.9 %all-to-all-done.2 = bf16[32,16,256]{2,0,1:T(8,128)(2,1)S(1)} async-done(((bf16[32,16,256]{2,0,1:T(8,128)(2,1)}), bf16[32,16,256]{2,0,1:T(8,128)(2,1)S(1)}, u32[]{:S(2)}, u32[]{:S(2)}) %all-to-all-start.2) | async-done | bytes 262176 | tf_op jit(solution)/shard_map/all_to_all | solution.py:59
  54.3 3.5 fusion.69
  57.8 1.9 convolution_convert_fusion.2
  59.7 3.9 %convolution_convert_fusion = bf16[512,5120]{1,0:T(8,128)(2,1)} fusion(bf16[512,256]{0,1:T(8,128)(2,1)S(1)} %bitcast.62, bf16[256,5120]{1,0:T(8,128)(2,1)S(1)} %copy-done), kind=kOutput, calls=%fused_computation.3 | convolution fusion | flops 1344798720 | bytes 8126464 | tf_op jit(solution)/shard_map/dot_general | solution.py:106
  64.3 77.5 %reduce-scatter.3.cloned.1.call-done = bf16[32,5120]{1,0:T(8,128)(2,1)} async-done(((bf16[512,5120]{1,0:T(8,128)(2,1)}), bf16[32,5120]{1,0:T(8,128)(2,1)}) %reduce-scatter.3.cloned.1.call-update) | async-done | bytes 327696 | tf_op jit(solution)/shard_map/reduce_scatter | solution.py:105
  144.1 1.9 add_convert_fusion.1
  146.4 13.9 %all_gather.10 = bf16[64,320,16]{1,0,2:T(8,128)(2,1)S(1)} all-gather(bf16[8,320,16]{1,0,2:T(8,128)(2,1)S(1)} %copy.59), channel_id=1, replica_groups=mesh['req'=8,'mlp'=16] {'req'}, dimensions={0}, use_global_device_ids=true | all-gather | bytes 737280 | tf_op jit(solution)/shard_map/all_gather | solution.py:66
  160.6 2.8 fusion.12
  163.4 38.2 %all-gather.3.cloned.1.call-done = bf16[512,5120]{1,0:T(8,128)(2,1)} async-done(((bf16[32,5120]{1,0:T(8,128)(2,1)}), bf16[512,5120]{1,0:T(8,128)(2,1)}) %all-gather.3.cloned.1.call-update) | async-done | bytes 5242896 | tf_op jit(solution)/shard_map/all_gather | solution.py:113
  203.1 72.4 %psum.7 = bf16[512,16]{0,1:T(8,128)(2,1)S(1)} all-reduce(bf16[512,16]{0,1:T(8,128)(2,1)S(1)} %fusion.15), channel_id=1, replica_groups=mesh['req'=8,'mlp'=16] {'mlp'}, use_global_device_ids=true, to_apply=%region_9.10 | all-reduce | flops 8192 | bytes 32768 | tf_op jit(solution)/shard_map/psum | solution.py:123
  275.5 11.1 %fusion.74 = f32[512,864]{0,1:T(8,128)} fusion(bf16[512,5120]{1,0:T(8,128)(2,1)} %all-gather.3.cloned.1.call-done, bf16[5120,864]{0,1:T(8,128)(2,1)} %param.22), kind=kOutput, calls=%fused_computation.79 | convolution fusion | flops 4529848320 | bytes 15859712 | tf_op jit(solution)/shard_map/dot_general | solution.py:128
  286.6 11.6 %convolution_convert_fusion.1 = bf16[512,5120]{1,0:T(8,128)(2,1)} fusion(bf16[864,5120]{1,0:T(8,128)(2,1)} %param.23, f32[512,864]{0,1:T(8,128)} %fusion.74, bf16[16,16,864]{2,0,1:T(8,128)(2,1)} %fusion.12, bf16[512,16]{0,1:T(8,128)(2,1)S(1)} %psum.7, bf16[512,16]{0,1:T(8,128)(2,1)S(1)} %get-tuple-element.3), kind=kOutput, calls=%fused_computation.4 | convolution fusion | flops 4763516928 | bytes 16334848 | tf_op jit(solution)/shard_map/dot_general | solution.py:134
  298.8 2.2 scatter_fusion
  301.0 2.4 scatter_fusion.1
  303.4 71.3 %reduce-scatter.5.cloned.1.call-done = bf16[32,5120]{1,0:T(8,128)(2,1)} async-done(((bf16[512,5120]{1,0:T(8,128)(2,1)}), bf16[32,5120]{1,0:T(8,128)(2,1)}) %reduce-scatter.5.cloned.1.call-update) | async-done | bytes 327696 | tf_op jit(solution)/shard_map/reduce_scatter | solution.py:133
  374.6 1.8 add_convert_fusion
  (53 shorter events, 11.0 us)
Async XLA Ops:
  8.0 51.7 %copy-start = (bf16[256,5120]{1,0:T(8,128)(2,1)S(1)}, bf16[256,5120]{1,0:T(8,128)(2,1)}, u32[]{:S(2)}) copy-start(bf16[256,5120]{1,0:T(8,128)(2,1)} %param.21) | copy-start | bytes 7864324
  8.0 13.5 %copy-start.4 = (bf16[32,4096]{1,0:T(8,128)(2,1)S(1)}, bf16[32,4096]{1,0:T(8,128)(2,1)}, u32[]{:S(2)}) copy-start(bf16[32,4096]{1,0:T(8,128)(2,1)} %param.17) | copy-start | bytes 786436
  8.0 25.6 %copy-start.8 = (s32[1,16]{1,0:T(1,128)S(1)}, s32[1,16]{1,0:T(1,128)}, u32[]{:S(2)}) copy-start(s32[1,16]{1,0:T(1,128)} %param.30) | copy-start | bytes 196
  13.3 16.7 %all-to-all-start.1 = ((bf16[32,16,256]{2,0,1:T(8,128)(2,1)}), bf16[32,16,256]{2,0,1:T(8,128)(2,1)S(1)}, u32[]{:S(2)}, u32[]{:S(2)}) async-start(bf16[32,16,256]{2,0,1:T(8,128)(2,1)} %bitcast.53), calls=%async_computation.1 | async-start | bytes 524288 | tf_op jit(solution)/shard_map/all_to_all | solution.py:58
  30.0 12.1 %all-to-all-start = ((bf16[32,16,256]{2,0,1:T(8,128)(2,1)}), bf16[32,16,256]{2,0,1:T(8,128)(2,1)S(1)}, u32[]{:S(2)}, u32[]{:S(2)}) async-start(bf16[32,16,256]{2,0,1:T(8,128)(2,1)} %bitcast.54), calls=%async_computation | async-start | bytes 524288 | tf_op jit(solution)/shard_map/all_to_all | solution.py:57
  42.1 12.1 %all-to-all-start.2 = ((bf16[32,16,256]{2,0,1:T(8,128)(2,1)}), bf16[32,16,256]{2,0,1:T(8,128)(2,1)S(1)}, u32[]{:S(2)}, u32[]{:S(2)}) async-start(bf16[32,16,256]{2,0,1:T(8,128)(2,1)} %bitcast.61), calls=%async_computation.2 | async-start | bytes 524288 | tf_op jit(solution)/shard_map/all_to_all | solution.py:59
  45.8 96.0 %reduce-scatter.3.cloned.1.call-start = ((), (), s32[]{:S(2)}) async-start(), calls=%async_computation.5 | async-start | bytes 5570560 | tf_op jit(solution)/shard_map/reduce_scatter | solution.py:105
  54.2 3.5 copy-start.3
  63.6 78.2 %copy-start.1 = (bf16[32,5120]{1,0:T(8,128)(2,1)S(1)}, bf16[32,5120]{1,0:T(8,128)(2,1)}, u32[]{:S(2)}) copy-start(bf16[32,5120]{1,0:T(8,128)(2,1)} %param.20) | copy-start | bytes 983044
  63.6 80.6 %copy-start.6 = (f32[5120]{0:T(1024)S(1)}, f32[5120]{0:T(1024)}, u32[]{:S(2)}) copy-start(f32[5120]{0:T(1024)} %param.25) | copy-start | bytes 61444
  63.6 80.6 %copy-start.7 = (f32[5120]{0:T(1024)S(1)}, f32[5120]{0:T(1024)}, u32[]{:S(2)}) copy-start(f32[5120]{0:T(1024)} %param.24) | copy-start | bytes 61444
  63.6 82.5 %copy-start.5 = (bf16[8,320,16]{1,2,0:T(8,128)(2,1)S(1)}, bf16[8,320,16]{1,2,0:T(8,128)(2,1)}, u32[]{:S(2)}) copy-start(bf16[8,320,16]{1,2,0:T(8,128)(2,1)} %param.26) | copy-start | bytes 245764
  63.6 82.5 %copy-start.9 = (s32[64]{0:T(128)S(1)}, s32[64]{0:T(128)}, u32[]{:S(2)}) copy-start(s32[64]{0:T(128)} %param.33) | copy-start | bytes 772
  63.6 82.5 %copy-start.10 = (s32[1,16]{1,0:T(1,128)S(1)}, s32[1,16]{1,0:T(1,128)}, u32[]{:S(2)}) copy-start(s32[1,16]{1,0:T(1,128)} %param.32) | copy-start | bytes 196
  63.6 97.0 %all-gather.5.cloned.1.call-start = ((), (), s32[]{:S(2)}) async-start(), calls=%async_computation.7 | async-start | bytes 2064384 | tf_op jit(solution)/shard_map/all_gather | solution.py:67
  64.2 137.4 %all-gather.3.cloned.1.call-start = ((), (), s32[]{:S(2)}) async-start(), calls=%async_computation.6 | async-start | bytes 5570560 | tf_op jit(solution)/shard_map/all_gather | solution.py:113
  146.1 228.6 %reduce-scatter.5.cloned.1.call-start = ((), (), s32[]{:S(2)}) async-start(), calls=%async_computation.8 | async-start | bytes 5570560 | tf_op jit(solution)/shard_map/reduce_scatter | solution.py:133
  298.1 0.7 copy-start.11
  298.1 76.5 %copy-start.2 = (bf16[32,5120]{1,0:T(8,128)(2,1)S(1)}, bf16[32,5120]{1,0:T(8,128)(2,1)}, u32[]{:S(2)}) copy-start(bf16[32,5120]{1,0:T(8,128)(2,1)} %reduce-scatter.3.cloned.1.call-done) | copy-start | bytes 983044
Sparse Core Ops, SparseCore 0:
  63.7 77.9 reduce-scatter.2
  298.3 76.3 reduce-scatter.4
Sparse Core Ops, SparseCore 1:
  65.8 22.7 all-gather.4
  146.1 55.4 all-gather.2
where the time goes:
time: 385 us; the launch traced here: 384 us
  waiting for transfers between devices  208 us (54%)
  blocking collectives  86.3 us (22%)
  matrix products  36.4 us (9%)
  between operations  15.7 us (4%)
  starting transfers between devices  15.6 us (4%)
  local copies, waits for them, and re-layouts  14.6 us (4%)
  other arithmetic  7.44 us (2%)
    reduce_scatter x1, waiting for transfers between devices, shards(): lax.psum_scatter(jnp.dot(row_block, attention_out_weight, preferred_eleme...  77.5 us
    psum x1, blocking collectives, shards(): lowrank = lax.psum(own_rank.astype(jnp.bfloat16), 'mlp')  72.4 us
    reduce_scatter x1, waiting for transfers between devices, shards(): lax.psum_scatter(jnp.dot(row_block, feedfwd_out_weight, preferred_element...  71.3 us
    all_gather x1, waiting for transfers between devices, shards(): lax.all_gather(modulate(residual, norm_gain_vector, norm_bias_vector), 'm...  38.2 us
    all_gather x1, blocking collectives, shards(): lax.all_gather(adapter_down_factors, 'req', axis=0, tiled=True)  13.9 us
    dot_general x1, matrix products, shards(): jnp.dot(row_block, feedfwd_out_weight, preferred_element_type=jnp.float32)  11.6 us
    dot_general x1, matrix products, shards(): jnp.dot(normed_all, feedfwd_in_weight, preferred_element_type=jnp.float32)  11.1 us
    all_to_all x1, starting transfers between devices, shards(): lax.all_to_all(keys, 'mlp', split_axis=1, concat_axis=0, tiled=True)  8.16 us
  transfers between devices with their start and end apart: 7, of which 6 were waited for; matrix products, arithmetic and copies ran while one was open for 5% of the time, Pallas kernels for 0%

commit v1 on v0

v1 whole, which is shorter than its diff:
```python
import functools

import jax
import jax.numpy as jnp
from jax import lax
from jax.experimental import pallas as pl
from jax.experimental.pallas import tpu as pltpu
from jax.sharding import PartitionSpec as P

MESH = pl.DeviceIdType.MESH
HS = 128
RANK = 16
REQS = 16
TOK_G = 512
WIDTH = 5120
HALF = WIDTH // 2
QUART = HALF // 2
UNITS = 864
HEADC = 256
TILE = 512
EPS = 1e-06
F32 = jnp.float32
BF16 = jnp.bfloat16

RELAY_F, RELAY_B, DIR_F, DIR_B, SUM_F, SUM_B = range(6)
R2F, R2B, F2F, F2B = range(24, 28)


def nt_dot(a, b):
    return lax.dot_general(a, b, (((1,), (1,)), ((), ())), preferred_element_type=F32)


def kernel(
    q_hbm, k_hbm, v_hbm, hid_hbm, wo_hbm, wi_hbm, w2_hbm, gain_hbm, bias_hbm, down_hbm, up_hbm, kc_hbm, vc_hbm,
    lens, look, adp, slot,
    out_hbm, ko_hbm, vo_hbm,
    qkv, att, wo, wi, w2, hid, gain, bias, downs, ups, kc, vc, start_col,
    part, norm, relay_f, relay_b, full_f, full_b, mid, relay2_f, relay2_b, full2_f, full2_b,
    resid, total, acc, act, onehot, dsel_f, dsel, usel, low, spread, outb,
    local_sem, a2a_send, a2a_recv, fac_send, fac_recv, low_send, low_recv, rs_send, rs_recv, ag_send, ag_recv,
):
    m = lax.axis_index("mlp")
    r = lax.axis_index("req")
    y, z = lax.div(m, 4), lax.rem(m, 4)

    def place(h, p, s):
        return (p, s) if h == 0 else (s, p)

    def device(h, p, s):
        a, b = place(h, p, s)
        return {"mlp": a * 4 + b}

    prim = (y, z)
    sec = (z, y)

    def up1(i, by):
        return lax.rem(i + by, 4)

    locals_ = {}

    def local(i, src, dst):
        c = pltpu.make_async_copy(src, dst, local_sem.at[i])
        c.start()
        locals_[i] = c

    local(0, wo_hbm, wo)
    local(3, hid_hbm, hid)
    local(4, gain_hbm, gain)
    local(5, bias_hbm, bias)
    local(6, kc_hbm, kc)
    local(7, vc_hbm, vc)
    local(8, down_hbm, downs.at[r])
    local(9, up_hbm, ups.at[r])
    for t, ref in enumerate((q_hbm, k_hbm, v_hbm)):
        cols = pl.ds(pl.multiple_of(m * HEADC, HEADC), HEADC)
        rows = pl.ds(pl.multiple_of(m * 32, 32), 32)
        local(10 + t, ref.at[:, cols], qkv.at[t, rows, :])

    barrier = pltpu.get_barrier_semaphore()

    def greet_mlp(i, c):
        pl.semaphore_signal(barrier, inc=1, device_id={"mlp": lax.rem(m + i, 16)}, device_id_type=MESH)
        return c

    def greet_req(i, c):
        pl.semaphore_signal(barrier, inc=1, device_id={"req": lax.rem(r + i, 8)}, device_id_type=MESH)
        return c

    lax.fori_loop(1, 16, greet_mlp, 0)
    lax.fori_loop(1, 8, greet_req, 0)
    pl.semaphore_wait(barrier, 22)

    def a2a_copy(t, ref, i):
        d = lax.rem(m + i, 16)
        return pltpu.make_async_remote_copy(
            src_ref=ref.at[:, pl.ds(pl.multiple_of(d * HEADC, HEADC), HEADC)],
            dst_ref=qkv.at[t, pl.ds(pl.multiple_of(m * 32, 32), 32), :],
            send_sem=a2a_send.at[t, i],
            recv_sem=a2a_recv.at[t, i],
            device_id={"mlp": d},
            device_id_type=MESH,
        )

    def a2a_start(i, c):
        for t, ref in enumerate((q_hbm, k_hbm, v_hbm)):
            a2a_copy(t, ref, i).start()
        return c

    lax.fori_loop(1, 16, a2a_start, 0)

    def fac_copy(t, src, dst, i):
        return pltpu.make_async_remote_copy(
            src_ref=src,
            dst_ref=dst.at[r],
            send_sem=fac_send.at[t, i],
            recv_sem=fac_recv.at[t, i],
            device_id={"req": lax.rem(r + i, 8)},
            device_id_type=MESH,
        )

    def fac_start(i, c):
        fac_copy(0, down_hbm, downs, i).start()
        fac_copy(1, up_hbm, ups, i).start()
        return c

    lax.fori_loop(1, 8, fac_start, 0)
    local(1, wi_hbm, wi)
    local(2, w2_hbm, w2)

    pos = lax.broadcasted_iota(jnp.int32, (TOK_G, 1), 0)
    starts, ends = [], []
    first = jnp.zeros((TOK_G, 1), jnp.int32)
    end = jnp.int32(0)
    for i in range(REQS):
        starts.append(end)
        end = end + lens[0, i]
        ends.append(end)
        first = jnp.where(pos >= end, end, first)
    start_col[...] = first

    for i in range(REQS):
        wanted = slot[adp[0, i]] * RANK
        lane = lax.broadcasted_iota(jnp.int32, (RANK, 64 * RANK), 1)
        sub = lax.broadcasted_iota(jnp.int32, (RANK, 64 * RANK), 0)
        onehot[i * RANK : (i + 1) * RANK, :] = (lane - sub == wanted).astype(F32).astype(BF16)
    acc[...] = jnp.zeros_like(acc)

    for t in range(3):
        locals_[10 + t].wait()

    def a2a_wait(i, c):
        for t, ref in enumerate((q_hbm, k_hbm, v_hbm)):
            a2a_copy(t, ref, i).wait_recv()
        return c

    lax.fori_loop(1, 16, a2a_wait, 0)

    for h in range(2):
        hc = slice(h * HS, (h + 1) * HS)
        for i in range(4):
            rows, length = slice(i * 128, (i + 1) * 128), (i + 1) * 128
            score = nt_dot(qkv[0, rows, hc], qkv[1, :length, hc]) * (HS ** (-0.5))
            qi = lax.broadcasted_iota(jnp.int32, (128, length), 0) + i * 128
            kj = lax.broadcasted_iota(jnp.int32, (128, length), 1)
            allowed = (kj <= qi) & (kj >= start_col[rows, :])
            score = jnp.where(allowed, score, -1e30)
            expo = jnp.exp(score - jnp.max(score, axis=1, keepdims=True))
            weights = (expo / jnp.sum(expo, axis=1, keepdims=True)).astype(BF16)
            mixed = jnp.dot(weights, qkv[2, :length, hc], preferred_element_type=F32)
            att[i, :, :, hc] = mixed.astype(BF16).reshape(4, 32, HS)

    def remote(src, dst, sems, h, i, dev):
        c = pltpu.make_async_remote_copy(
            src_ref=src,
            dst_ref=dst,
            send_sem=sems[0].at[h, i],
            recv_sem=sems[1].at[h, i],
            device_id=dev,
            device_id_type=MESH,
        )
        c.start()
        return c

    def cols_of(h, which):
        base = h * HALF
        if which == "F":
            return slice(base, base + QUART)
        if which == "B":
            return slice(base + QUART, base + HALF)
        return slice(base, base + HALF)

    def reduce_scatter(left, right, own, fill):
        flying = {}
        sems = (rs_send, rs_recv)

        def view(h, p, s, which):
            a, b = place(h, p, s)
            return part.at[a, b, :, cols_of(h, which)]

        def load(h, p, s, which):
            a, b = place(h, p, s)
            return part[a, b, :, cols_of(h, which)].astype(F32)

        def store(h, p, s, which, value):
            a, b = place(h, p, s)
            part[a, b, :, cols_of(h, which)] = value.astype(BF16)

        def order(h, k):
            return up1(sec[h], (2, 1, 3, 0)[k])

        def product(h, k):
            s = order(h, k)
            lhs = left[:, s] if h == 0 else left[s]
            lhs = lhs.reshape(128, left.shape[3])
            for c in range(h * HALF, (h + 1) * HALF, TILE):
                value = jnp.dot(lhs, right[:, c : c + TILE], preferred_element_type=F32).astype(BF16)
                value = value.reshape(4, 32, TILE)
                if h == 0:
                    part[:, s, :, c : c + TILE] = value
                else:
                    part[s, :, :, c : c + TILE] = value

        def first_sends(h, k):
            p, s, sp = prim[h], sec[h], order(h, k)
            ahead, behind = device(h, up1(p, 1), s), device(h, up1(p, 3), s)
            i = 6 * k
            far = up1(p, 2)
            flying[h, i + RELAY_F] = remote(view(h, far, sp, "F"), relay_f.at[h, k], sems, h, i + RELAY_F, ahead)
            flying[h, i + RELAY_B] = remote(view(h, far, sp, "B"), relay_b.at[h, k], sems, h, i + RELAY_B, behind)
            flying[h, i + DIR_F] = remote(
                view(h, up1(p, 1), sp, "B"), full_f.at[h, k, :, QUART:], sems, h, i + DIR_F, ahead
            )
            flying[h, i + DIR_B] = remote(
                view(h, up1(p, 3), sp, "F"), full_b.at[h, k, :, :QUART], sems, h, i + DIR_B, behind
            )

        def second_sends(h, k):
            p, s, sp = prim[h], sec[h], order(h, k)
            ahead, behind = device(h, up1(p, 1), s), device(h, up1(p, 3), s)
            i = 6 * k
            flying[h, i + RELAY_F].wait_recv()
            store(h, up1(p, 1), sp, "F", load(h, up1(p, 1), sp, "F") + relay_f[h, k].astype(F32))
            flying[h, i + SUM_F] = remote(
                view(h, up1(p, 1), sp, "F"), full_f.at[h, k, :, :QUART], sems, h, i + SUM_F, ahead
            )
            flying[h, i + RELAY_B].wait_recv()
            store(h, up1(p, 3), sp, "B", load(h, up1(p, 3), sp, "B") + relay_b[h, k].astype(F32))
            flying[h, i + SUM_B] = remote(
                view(h, up1(p, 3), sp, "B"), full_b.at[h, k, :, QUART:], sems, h, i + SUM_B, behind
            )

        def third_sends(h, k):
            p, s, sp = prim[h], sec[h], order(h, k)
            for name in (DIR_F, SUM_F, DIR_B, SUM_B):
                flying[h, 6 * k + name].wait_recv()
            value = load(h, p, sp, "W") + full_f[h, k].astype(F32) + full_b[h, k].astype(F32)
            ahead, behind = device(h, p, up1(s, 1)), device(h, p, up1(s, 3))
            if k == 0:
                mid[h, 0] = value.astype(BF16)
                flying[h, R2F] = remote(mid.at[h, 0, :, :QUART], relay2_f.at[h], sems, h, R2F, ahead)
                flying[h, R2B] = remote(mid.at[h, 0, :, QUART:], relay2_b.at[h], sems, h, R2B, behind)
            elif k == 1:
                flying[h, R2F].wait_recv()
                mid[h, 1, :, :QUART] = (value[:, :QUART] + relay2_f[h].astype(F32)).astype(BF16)
                mid[h, 1, :, QUART:] = value[:, QUART:].astype(BF16)
                flying[h, F2F] = remote(mid.at[h, 1], full2_f.at[h], sems, h, F2F, ahead)
            elif k == 2:
                flying[h, R2B].wait_recv()
                mid[h, 2, :, :QUART] = value[:, :QUART].astype(BF16)
                mid[h, 2, :, QUART:] = (value[:, QUART:] + relay2_b[h].astype(F32)).astype(BF16)
                flying[h, F2B] = remote(mid.at[h, 2], full2_b.at[h], sems, h, F2B, behind)
            else:
                own[:, cols_of(h, "W")] = value

        for k in range(4):
            for h in range(2):
                product(h, k)
                first_sends(h, k)
            if k >= 1:
                for h in range(2):
                    second_sends(h, k - 1)
            if k >= 2:
                for h in range(2):
                    third_sends(h, k - 2)
        for h in range(2):
            second_sends(h, 3)
        fill()
        for k in (2, 3):
            for h in range(2):
                third_sends(h, k)
        for h in range(2):
            flying[h, F2F].wait_recv()
            flying[h, F2B].wait_recv()
        for copy in flying.values():
            copy.wait_send()

    def pages():
        locals_[6].wait()
        locals_[7].wait()
        for t, cache, hbm in ((1, kc, ko_hbm), (2, vc, vo_hbm)):
            for page in range(5):
                value = cache[page]
                for b in range(4):
                    value = jnp.where(look[0, b] == page, qkv[t, b * 128 : (b + 1) * 128, :], value)
                cache[page] = value
            local(12 + t, cache, hbm)

    locals_[0].wait()
    locals_[3].wait()
    reduce_scatter(att, wo, total, pages)

    for h in range(2):
        cs = cols_of(h, "W")
        resid[:, cs] = (
            hid[:, cs].astype(F32) + total[:, cs] + full2_f[h].astype(F32) + full2_b[h].astype(F32)
        )
    locals_[4].wait()
    locals_[5].wait()
    mean = jnp.sum(resid[...], axis=1, keepdims=True) * (1.0 / WIDTH)
    centered = resid[...] - mean
    var = jnp.sum(centered * centered, axis=1, keepdims=True) * (1.0 / WIDTH)
    norm[y, z] = (centered * lax.rsqrt(var + EPS) * gain[...] + bias[...]).astype(BF16)

    flying = {}
    ag = (ag_send, ag_recv)
    OWN_F, OWN_B, REL_F, REL_B = range(4)

    def nview(h, p, s, which):
        a, b = place(h, p, s)
        return norm.at[a, b, :, cols_of(h, which)]

    def ag1(h, i, sp, which, by):
        p, s = prim[h], sec[h]
        ref = nview(h, p, sp, which)
        flying[h, i] = remote(ref, ref, ag, h, i, device(h, p, up1(s, by)))

    def ag2(h, k, i, pp, which, by):
        p, s = prim[h], sec[h]
        ref = nview(h, pp, up1(s, (0, 3, 1, 2)[k]), which)
        flying[h, 4 + 4 * k + i] = remote(ref, ref, ag, h, 4 + 4 * k + i, device(h, up1(p, by), s))

    def ag2_own(h, k):
        ag2(h, k, OWN_F, prim[h], "W", 1)
        ag2(h, k, OWN_B, prim[h], "W", 3)

    def ag2_relay(h, k):
        flying[h, 4 + 4 * k + OWN_F].wait_recv()
        ag2(h, k, REL_F, up1(prim[h], 3), "F", 1)
        flying[h, 4 + 4 * k + OWN_B].wait_recv()
        ag2(h, k, REL_B, up1(prim[h], 1), "B", 3)

    def ag2_done(h, k):
        flying[h, 4 + 4 * k + REL_F].wait_recv()
        flying[h, 4 + 4 * k + REL_B].wait_recv()

    def in_product(h, k):
        sp = up1(sec[h], (0, 3, 1, 2)[k])
        cs = cols_of(h, "W")
        lhs = norm[:, sp, :, cs] if h == 0 else norm[sp, :, :, cs]
        value = nt_dot(lhs.reshape(128, HALF), wi[:, cs]).reshape(4, 32, UNITS)
        if h == 0:
            acc[:, sp] = acc[:, sp] + value
        else:
            acc[sp] = acc[sp] + value

    for h in range(2):
        ag1(h, OWN_F, sec[h], "W", 1)
        ag1(h, OWN_B, sec[h], "W", 3)
    for h in range(2):
        ag2_own(h, 0)

    def fac_wait(i, c):
        fac_copy(0, down_hbm, downs, i).wait()
        fac_copy(1, up_hbm, ups, i).wait()
        return c

    locals_[8].wait()
    locals_[9].wait()
    lax.fori_loop(1, 8, fac_wait, 0)

    for h in range(2):
        flying[h, OWN_F].wait_recv()
        ag1(h, REL_F, up1(sec[h], 3), "F", 1)
        ag2_own(h, 1)
        flying[h, OWN_B].wait_recv()
        ag1(h, REL_B, up1(sec[h], 1), "B", 3)
        ag2_own(h, 2)

    picked = jnp.dot(onehot[...], downs[...].reshape(64 * RANK, 320), preferred_element_type=F32)
    dsel_f[...] = jnp.zeros_like(dsel_f)
    dsel_f[:, :320] = picked
    shifted = jnp.where(lax.rem(m, 2) == 1, pltpu.roll(dsel_f[...], 64, 1), dsel_f[...])
    dsel[...] = shifted.astype(BF16)

    for h in range(2):
        ag2_relay(h, 0)
    for h in range(2):
        flying[h, REL_F].wait_recv()
        flying[h, REL_B].wait_recv()
        ag2_own(h, 3)
    usel[...] = jnp.dot(onehot[...], ups[...].reshape(64 * RANK, UNITS), preferred_element_type=F32).astype(BF16)
    locals_[1].wait()
    for k in range(1, 4):
        for h in range(2):
            ag2_relay(h, k)
        for h in range(2):
            ag2_done(h, k - 1)
            in_product(h, k - 1)
    for h in range(2):
        ag2_done(h, 3)

    window = pl.ds(pl.multiple_of(lax.div(m * 5 - lax.rem(m, 2), 2) * 128, 128), 384)
    ranks = nt_dot(dsel[...], norm[:, :, :, window].reshape(TOK_G, 384))
    token = lax.broadcasted_iota(jnp.int32, (RANK, TOK_G), 1)
    mine = jnp.zeros((RANK, TOK_G), F32)
    for i in range(REQS):
        inside = (token >= starts[i]) & (token < ends[i])
        mine = mine + jnp.where(inside, ranks[i * RANK : (i + 1) * RANK, :], 0.0)
    low[m] = mine.astype(BF16)

    def low_copy(i):
        return pltpu.make_async_remote_copy(
            src_ref=low.at[m],
            dst_ref=low.at[m],
            send_sem=low_send.at[i],
            recv_sem=low_recv.at[i],
            device_id={"mlp": lax.rem(m + i, 16)},
            device_id_type=MESH,
        )

    def low_start(i, c):
        low_copy(i).start()
        return c

    lax.fori_loop(1, 16, low_start, 0)
    for h in range(2):
        in_product(h, 3)

    def low_wait(i, c):
        low_copy(i).wait()
        return c

    lax.fori_loop(1, 16, low_wait, 0)
    lowrank = jnp.sum(low[...].astype(F32), axis=0).astype(BF16).astype(F32)
    for i in range(REQS):
        inside = (token >= starts[i]) & (token < ends[i])
        spread[i * RANK : (i + 1) * RANK, :] = jnp.where(inside, lowrank, 0.0).astype(BF16)

    for i in range(4):
        adapted = lax.dot_general(
            spread[:, i * 128 : (i + 1) * 128], usel[...], (((0,), (0,)), ((), ())), preferred_element_type=F32
        )
        preact = acc[i] + adapted.reshape(4, 32, UNITS)
        act[i] = jax.nn.gelu(preact, approximate=True).astype(BF16)
    for copy in flying.values():
        copy.wait_send()

    def nothing():
        return None

    locals_[2].wait()
    reduce_scatter(act, w2, total, nothing)
    for h in range(2):
        cs = cols_of(h, "W")
        value = resid[:, cs] + (total[:, cs] + full2_f[h].astype(F32) + full2_b[h].astype(F32))
        outb[:, cs] = value.astype(BF16)
    local(15, outb, out_hbm)

    def a2a_sent(i, c):
        for t, ref in enumerate((q_hbm, k_hbm, v_hbm)):
            a2a_copy(t, ref, i).wait_send()
        return c

    lax.fori_loop(1, 16, a2a_sent, 0)
    for i in (13, 14, 15):
        locals_[i].wait()


def shards(*args):
    (queries, keys, values, hidden, w_o, w_in, w_out, gain, bias, down, up, kc, vc, lens, look, adp, slot) = args
    any_, smem = pl.BlockSpec(memory_space=pl.ANY), pl.BlockSpec(memory_space=pltpu.SMEM)
    vmem, dma = pltpu.VMEM, pltpu.SemaphoreType.DMA
    scratch = [
        vmem((3, TOK_G, HEADC), BF16),
        vmem((4, 4, 32, HEADC), BF16),
        vmem((HEADC, WIDTH), BF16),
        vmem((UNITS, WIDTH), BF16),
        vmem((UNITS, WIDTH), BF16),
        vmem((32, WIDTH), BF16),
        vmem((1, WIDTH), F32),
        vmem((1, WIDTH), F32),
        vmem((8, 128, 320), BF16),
        vmem((8, 128, UNITS), BF16),
        vmem((5, 128, HEADC), BF16),
        vmem((5, 128, HEADC), BF16),
        vmem((TOK_G, 1), jnp.int32),
        vmem((4, 4, 32, WIDTH), BF16),
        vmem((4, 4, 32, WIDTH), BF16),
        vmem((2, 4, 32, QUART), BF16),
        vmem((2, 4, 32, QUART), BF16),
        vmem((2, 4, 32, HALF), BF16),
        vmem((2, 4, 32, HALF), BF16),
        vmem((2, 3, 32, HALF), BF16),
        vmem((2, 32, QUART), BF16),
        vmem((2, 32, QUART), BF16),
        vmem((2, 32, HALF), BF16),
        vmem((2, 32, HALF), BF16),
        vmem((32, WIDTH), F32),
        vmem((32, WIDTH), F32),
        vmem((4, 4, 32, UNITS), F32),
        vmem((4, 4, 32, UNITS), BF16),
        vmem((REQS * RANK, 64 * RANK), BF16),
        vmem((REQS * RANK, 384), F32),
        vmem((REQS * RANK, 384), BF16),
        vmem((REQS * RANK, UNITS), BF16),
        vmem((16, RANK, TOK_G), BF16),
        vmem((REQS * RANK, TOK_G), BF16),
        vmem((32, WIDTH), BF16),
        dma((16,)),
        dma((3, 16)),
        dma((3, 16)),
        dma((2, 8)),
        dma((2, 8)),
        dma((16,)),
        dma((16,)),
        dma((2, 28)),
        dma((2, 28)),
        dma((2, 20)),
        dma((2, 20)),
    ]
    return pl.pallas_call(
        kernel,
        out_shape=(
            jax.ShapeDtypeStruct((32, WIDTH), BF16),
            jax.ShapeDtypeStruct((5, 128, HEADC), BF16),
            jax.ShapeDtypeStruct((5, 128, HEADC), BF16),
        ),
        in_specs=[any_] * 13 + [smem] * 4,
        out_specs=(any_, any_, any_),
        scratch_shapes=scratch,
        compiler_params=pltpu.CompilerParams(
            collective_id=0, has_side_effects=True, vmem_limit_bytes=62 * 1024 * 1024
        ),
    )(
        queries, keys, values, hidden, w_o, w_in.T, w_out, gain.reshape(1, WIDTH), bias.reshape(1, WIDTH),
        jnp.transpose(down, (0, 2, 1)).reshape(128, 320), up.reshape(128, UNITS), kc, vc, lens, look, adp, slot,
    )


def solution(mesh):
    in_specs = (
        P(("req", "mlp"), None),
        P(("req", "mlp"), None),
        P(("req", "mlp"), None),
        P(("req", "mlp"), None),
        P("mlp", None),
        P(None, "mlp"),
        P("mlp", None),
        P(),
        P(),
        P("req", "mlp", None),
        P("req", None, "mlp"),
        P("req", None, "mlp"),
        P("req", None, "mlp"),
        P("req", None),
        P("req", None),
        P("req", None),
        P(),
    )
    out_specs = (P(("req", "mlp"), None), P("req", None, "mlp"), P("req", None, "mlp"))
    return jax.shard_map(shards, mesh=mesh, in_specs=in_specs, out_specs=out_specs, check_vma=False)
```

time: 385 us -> 131 us (0.34)
  waiting for transfers between devices: 208 us -> 0 us
  Pallas kernels: 0 us -> 125 us
  blocking collectives: 86.3 us -> 0 us
  matrix products: 36.4 us -> 0 us
  starting transfers between devices: 15.6 us -> 0 us
  between operations: 15.7 us -> 0.65 us
  local copies, waits for them, and re-layouts: 14.6 us -> 5.15 us
  other arithmetic: 7.44 us -> 0 us
    reduce_scatter x2 -> x0, waiting for transfers between devices: 149 us -> none  [the longest x1 77.5 us: shards(): lax.psum_scatter(jnp.dot(row_block, attention_out_weight, preferred_eleme...]
    pallas_call x0 -> x1, Pallas kernels: none -> 125 us  [shards(): pl.pallas_call(kernel, out_shape=(jax.ShapeDtypeStruct((32, WIDTH), BF16)...]
    psum x1 -> x0, blocking collectives: 72.4 us -> none  [shards(): lowrank = lax.psum(own_rank.astype(jnp.bfloat16), 'mlp')]
    all_gather x2 -> x0, waiting for transfers between devices: 38.2 us -> none  [the longest x1 38.2 us: shards(): lax.all_gather(modulate(residual, norm_gain_vector, norm_bias_vector), 'm...]
    dot_general x7 -> x0, matrix products: 33 us -> none  [the longest x1 11.6 us: shards(): jnp.dot(row_block, feedfwd_out_weight, preferred_element_type=jnp.float32)]
    all_to_all x3 -> x0, waiting for transfers between devices: 20.2 us -> none  [the longest x1 7.78 us: shards(): lax.all_to_all(keys, 'mlp', split_axis=1, concat_axis=0, tiled=True)]
    all_to_all x3 -> x0, starting transfers between devices: 15.5 us -> none  [the longest x1 8.16 us: shards(): lax.all_to_all(keys, 'mlp', split_axis=1, concat_axis=0, tiled=True)]
    all_gather x1 -> x0, blocking collectives: 13.9 us -> none  [shards(): lax.all_gather(adapter_down_factors, 'req', axis=0, tiled=True)]
  transfers between devices with their start and end apart: 7 -> 0, of which waited for: 6 -> 0; matrix products, arithmetic and copies ran while one was open for 5% -> 0% of each run, Pallas kernels for 0% -> 0%
where the time goes in v1:
time: 131 us
  Pallas kernels  125 us (95%)
  local copies, waits for them, and re-layouts  5.15 us (4%)
    pallas_call x1, Pallas kernels, shards(): pl.pallas_call(kernel, out_shape=(jax.ShapeDtypeStruct((32, WIDTH), BF16)...  125 us
    unnamed x3, local copies, waits for them, and re-layouts  5.15 us

profile of v1, /device:TPU:0, one launch (start us, length us, event | category | flops | bytes accessed | tf_op | source)
XLA Modules:
  0.0 130.9 jit_solution(15324644202934699338)
XLA Ops:
  0.6 125.1 %shard_map.184 = (bf16[32,5120]{1,0:T(8,128)(2,1)}, bf16[5,128,256]{2,1,0:T(8,128)(2,1)}, bf16[5,128,256]{2,1,0:T(8,128)(2,1)}) custom-call(bf16[32,4096]{1,0:T(8,128)(2,1)} %q_hbm.1, bf16[32,4096]{1,0:T(8,128)(2,1)} %k_hbm.1, bf16[32,4096]{1,0:T(8,128)(2,1)} %v_hbm.1, bf16[32,5120]{1,0:T(8,128)(2,1)} %hid_hbm.1, bf16[256,5120]{1,0:T(8,128)(2,1)} %wo_hbm.1, ...), custom_call_target="tpu_custom_call" | custom-call | tf_op jit(solution)/shard_map/pallas_call | solution.py:531
  125.7 1.7 %copy.23 = bf16[32,5120]{1,0:T(8,128)(2,1)} copy(bf16[32,5120]{1,0:T(8,128)(2,1)} %get-tuple-element.6) | data formatting | bytes 655360
  127.5 1.7 %copy.24 = bf16[5,128,256]{2,1,0:T(8,128)(2,1)} copy(bf16[5,128,256]{2,1,0:T(8,128)(2,1)} %get-tuple-element.7) | data formatting | bytes 655360
  129.2 1.7 %copy.25 = bf16[5,128,256]{2,1,0:T(8,128)(2,1)} copy(bf16[5,128,256]{2,1,0:T(8,128)(2,1)} %get-tuple-element.8) | data formatting | bytes 655360

commit v2 on v1

--- a/solution.py
+++ b/solution.py
@@ -22,8 +22,8 @@
 F32 = jnp.float32
 BF16 = jnp.bfloat16
 
-RELAY_F, RELAY_B, DIR_F, DIR_B, SUM_F, SUM_B = range(6)
-R2F, R2B, F2F, F2B = range(24, 28)
+RELAY_F, RELAY_B, FULL = range(3)
+R2F, R2B, FULL2 = range(12, 15)
 
 
 def nt_dot(a, b):
@@ -33,10 +33,10 @@
 def kernel(
     q_hbm, k_hbm, v_hbm, hid_hbm, wo_hbm, wi_hbm, w2_hbm, gain_hbm, bias_hbm, down_hbm, up_hbm, kc_hbm, vc_hbm,
     lens, look, adp, slot,
-    out_hbm, ko_hbm, vo_hbm,
+    outb, ko, vo,
     qkv, att, wo, wi, w2, hid, gain, bias, downs, ups, kc, vc, start_col,
     part, norm, relay_f, relay_b, full_f, full_b, mid, relay2_f, relay2_b, full2_f, full2_b,
-    resid, total, acc, act, onehot, dsel_f, dsel, usel, low, spread, outb,
+    resid, total, acc, act, onehot, dsel_f, dsel, usel, low, spread,
     local_sem, a2a_send, a2a_recv, fac_send, fac_recv, low_send, low_recv, rs_send, rs_recv, ag_send, ag_recv,
 ):
     m = lax.axis_index("mlp")
@@ -55,6 +55,9 @@
 
     def up1(i, by):
         return lax.rem(i + by, 4)
+
+    def wait_for(like, sem):
+        pltpu.make_async_copy(like, like, sem).wait()
 
     locals_ = {}
 
@@ -69,12 +72,12 @@
     local(5, bias_hbm, bias)
     local(6, kc_hbm, kc)
     local(7, vc_hbm, vc)
-    local(8, down_hbm, downs.at[r])
-    local(9, up_hbm, ups.at[r])
+    pltpu.make_async_copy(down_hbm, downs.at[r], fac_recv.at[0]).start()
+    pltpu.make_async_copy(up_hbm, ups.at[r], fac_recv.at[1]).start()
     for t, ref in enumerate((q_hbm, k_hbm, v_hbm)):
         cols = pl.ds(pl.multiple_of(m * HEADC, HEADC), HEADC)
         rows = pl.ds(pl.multiple_of(m * 32, 32), 32)
-        local(10 + t, ref.at[:, cols], qkv.at[t, rows, :])
+        pltpu.make_async_copy(ref.at[:, cols], qkv.at[t, rows, :], a2a_recv.at[0]).start()
 
     barrier = pltpu.get_barrier_semaphore()
 
@@ -95,8 +98,8 @@
         return pltpu.make_async_remote_copy(
             src_ref=ref.at[:, pl.ds(pl.multiple_of(d * HEADC, HEADC), HEADC)],
             dst_ref=qkv.at[t, pl.ds(pl.multiple_of(m * 32, 32), 32), :],
-            send_sem=a2a_send.at[t, i],
-            recv_sem=a2a_recv.at[t, i],
+            send_sem=a2a_send.at[0],
+            recv_sem=a2a_recv.at[0],
             device_id={"mlp": d},
             device_id_type=MESH,
         )
@@ -112,8 +115,8 @@
         return pltpu.make_async_remote_copy(
             src_ref=src,
             dst_ref=dst.at[r],
-            send_sem=fac_send.at[t, i],
-            recv_sem=fac_recv.at[t, i],
+            send_sem=fac_send.at[t],
+            recv_sem=fac_recv.at[t],
             device_id={"req": lax.rem(r + i, 8)},
             device_id_type=MESH,
         )
@@ -145,15 +148,7 @@
         onehot[i * RANK : (i + 1) * RANK, :] = (lane - sub == wanted).astype(F32).astype(BF16)
     acc[...] = jnp.zeros_like(acc)
 
-    for t in range(3):
-        locals_[10 + t].wait()
-
-    def a2a_wait(i, c):
-        for t, ref in enumerate((q_hbm, k_hbm, v_hbm)):
-            a2a_copy(t, ref, i).wait_recv()
-        return c
-
-    lax.fori_loop(1, 16, a2a_wait, 0)
+    wait_for(qkv, a2a_recv.at[0])
 
     for h in range(2):
         hc = slice(h * HS, (h + 1) * HS)
@@ -173,7 +168,7 @@
         c = pltpu.make_async_remote_copy(
             src_ref=src,
             dst_ref=dst,
-            send_sem=sems[0].at[h, i],
+            send_sem=sems[0].at[h],
             recv_sem=sems[1].at[h, i],
             device_id=dev,
             device_id_type=MESH,
@@ -223,36 +218,27 @@
         def first_sends(h, k):
             p, s, sp = prim[h], sec[h], order(h, k)
             ahead, behind = device(h, up1(p, 1), s), device(h, up1(p, 3), s)
-            i = 6 * k
+            i = 3 * k
             far = up1(p, 2)
             flying[h, i + RELAY_F] = remote(view(h, far, sp, "F"), relay_f.at[h, k], sems, h, i + RELAY_F, ahead)
             flying[h, i + RELAY_B] = remote(view(h, far, sp, "B"), relay_b.at[h, k], sems, h, i + RELAY_B, behind)
-            flying[h, i + DIR_F] = remote(
-                view(h, up1(p, 1), sp, "B"), full_f.at[h, k, :, QUART:], sems, h, i + DIR_F, ahead
-            )
-            flying[h, i + DIR_B] = remote(
-                view(h, up1(p, 3), sp, "F"), full_b.at[h, k, :, :QUART], sems, h, i + DIR_B, behind
-            )
+            remote(view(h, up1(p, 1), sp, "B"), full_f.at[h, k, :, QUART:], sems, h, i + FULL, ahead)
+            remote(view(h, up1(p, 3), sp, "F"), full_b.at[h, k, :, :QUART], sems, h, i + FULL, behind)
 
         def second_sends(h, k):
             p, s, sp = prim[h], sec[h], order(h, k)
             ahead, behind = device(h, up1(p, 1), s), device(h, up1(p, 3), s)
-            i = 6 * k
+            i = 3 * k
             flying[h, i + RELAY_F].wait_recv()
             store(h, up1(p, 1), sp, "F", load(h, up1(p, 1), sp, "F") + relay_f[h, k].astype(F32))
-            flying[h, i + SUM_F] = remote(
-                view(h, up1(p, 1), sp, "F"), full_f.at[h, k, :, :QUART], sems, h, i + SUM_F, ahead
-            )
+            remote(view(h, up1(p, 1), sp, "F"), full_f.at[h, k, :, :QUART], sems, h, i + FULL, ahead)
             flying[h, i + RELAY_B].wait_recv()
             store(h, up1(p, 3), sp, "B", load(h, up1(p, 3), sp, "B") + relay_b[h, k].astype(F32))
-            flying[h, i + SUM_B] = remote(
-                view(h, up1(p, 3), sp, "B"), full_b.at[h, k, :, QUART:], sems, h, i + SUM_B, behind
-            )
+            remote(view(h, up1(p, 3), sp, "B"), full_b.at[h, k, :, QUART:], sems, h, i + FULL, behind)
 
         def third_sends(h, k):
             p, s, sp = prim[h], sec[h], order(h, k)
-            for name in (DIR_F, SUM_F, DIR_B, SUM_B):
-                flying[h, 6 * k + name].wait_recv()
+            wait_for(wo.at[0:32], rs_recv.at[h, 3 * k + FULL])
             value = load(h, p, sp, "W") + full_f[h, k].astype(F32) + full_b[h, k].astype(F32)
             ahead, behind = device(h, p, up1(s, 1)), device(h, p, up1(s, 3))
             if k == 0:
@@ -263,12 +249,12 @@
                 flying[h, R2F].wait_recv()
                 mid[h, 1, :, :QUART] = (value[:, :QUART] + relay2_f[h].astype(F32)).astype(BF16)
                 mid[h, 1, :, QUART:] = value[:, QUART:].astype(BF16)
-                flying[h, F2F] = remote(mid.at[h, 1], full2_f.at[h], sems, h, F2F, ahead)
+                remote(mid.at[h, 1], full2_f.at[h], sems, h, FULL2, ahead)
             elif k == 2:
                 flying[h, R2B].wait_recv()
                 mid[h, 2, :, :QUART] = value[:, :QUART].astype(BF16)
                 mid[h, 2, :, QUART:] = (value[:, QUART:] + relay2_b[h].astype(F32)).astype(BF16)
-                flying[h, F2B] = remote(mid.at[h, 2], full2_b.at[h], sems, h, F2B, behind)
+                remote(mid.at[h, 2], full2_b.at[h], sems, h, FULL2, behind)
             else:
                 own[:, cols_of(h, "W")] = value
 
@@ -289,21 +275,19 @@
             for h in range(2):
                 third_sends(h, k)
         for h in range(2):
-            flying[h, F2F].wait_recv()
-            flying[h, F2B].wait_recv()
-        for copy in flying.values():
-            copy.wait_send()
+            wait_for(wo.at[0:32], rs_recv.at[h, FULL2])
+        for h in range(2):
+            wait_for(wo.at[0:240], rs_send.at[h])
 
     def pages():
         locals_[6].wait()
         locals_[7].wait()
-        for t, cache, hbm in ((1, kc, ko_hbm), (2, vc, vo_hbm)):
+        for t, cache, out in ((1, kc, ko), (2, vc, vo)):
             for page in range(5):
                 value = cache[page]
                 for b in range(4):
                     value = jnp.where(look[0, b] == page, qkv[t, b * 128 : (b + 1) * 128, :], value)
-                cache[page] = value
-            local(12 + t, cache, hbm)
+                out[page] = value
 
     locals_[0].wait()
     locals_[3].wait()
@@ -323,7 +307,7 @@
 
     flying = {}
     ag = (ag_send, ag_recv)
-    OWN_F, OWN_B, REL_F, REL_B = range(4)
+    OWN_F, OWN_B, REL = range(3)
 
     def nview(h, p, s, which):
         a, b = place(h, p, s)
@@ -337,21 +321,20 @@
     def ag2(h, k, i, pp, which, by):
         p, s = prim[h], sec[h]
         ref = nview(h, pp, up1(s, (0, 3, 1, 2)[k]), which)
-        flying[h, 4 + 4 * k + i] = remote(ref, ref, ag, h, 4 + 4 * k + i, device(h, up1(p, by), s))
+        flying[h, 3 + 3 * k + i] = remote(ref, ref, ag, h, 3 + 3 * k + i, device(h, up1(p, by), s))
 
     def ag2_own(h, k):
         ag2(h, k, OWN_F, prim[h], "W", 1)
         ag2(h, k, OWN_B, prim[h], "W", 3)
 
     def ag2_relay(h, k):
-        flying[h, 4 + 4 * k + OWN_F].wait_recv()
-        ag2(h, k, REL_F, up1(prim[h], 3), "F", 1)
-        flying[h, 4 + 4 * k + OWN_B].wait_recv()
-        ag2(h, k, REL_B, up1(prim[h], 1), "B", 3)
+        flying[h, 3 + 3 * k + OWN_F].wait_recv()
+        ag2(h, k, REL, up1(prim[h], 3), "F", 1)
+        flying[h, 3 + 3 * k + OWN_B].wait_recv()
+        ag2(h, k, REL, up1(prim[h], 1), "B", 3)
 
     def ag2_done(h, k):
-        flying[h, 4 + 4 * k + REL_F].wait_recv()
-        flying[h, 4 + 4 * k + REL_B].wait_recv()
+        wait_for(wo.at[0:16], ag_recv.at[h, 3 + 3 * k + REL])
 
     def in_product(h, k):
         sp = up1(sec[h], (0, 3, 1, 2)[k])
@@ -369,21 +352,16 @@
     for h in range(2):
         ag2_own(h, 0)
 
-    def fac_wait(i, c):
-        fac_copy(0, down_hbm, downs, i).wait()
-        fac_copy(1, up_hbm, ups, i).wait()
-        return c
-
-    locals_[8].wait()
-    locals_[9].wait()
-    lax.fori_loop(1, 8, fac_wait, 0)
+    for t, ref in enumerate((downs, ups)):
+        wait_for(ref, fac_recv.at[t])
+        wait_for(ref.at[0:7], fac_send.at[t])
 
     for h in range(2):
         flying[h, OWN_F].wait_recv()
-        ag1(h, REL_F, up1(sec[h], 3), "F", 1)
+        ag1(h, REL, up1(sec[h], 3), "F", 1)
         ag2_own(h, 1)
         flying[h, OWN_B].wait_recv()
-        ag1(h, REL_B, up1(sec[h], 1), "B", 3)
+        ag1(h, REL, up1(sec[h], 1), "B", 3)
         ag2_own(h, 2)
 
     picked = jnp.dot(onehot[...], downs[...].reshape(64 * RANK, 320), preferred_element_type=F32)
@@ -395,8 +373,7 @@
     for h in range(2):
         ag2_relay(h, 0)
     for h in range(2):
-        flying[h, REL_F].wait_recv()
-        flying[h, REL_B].wait_recv()
+        wait_for(wo.at[0:16], ag_recv.at[h, REL])
         ag2_own(h, 3)
     usel[...] = jnp.dot(onehot[...], ups[...].reshape(64 * RANK, UNITS), preferred_element_type=F32).astype(BF16)
     locals_[1].wait()
@@ -422,8 +399,8 @@
         return pltpu.make_async_remote_copy(
             src_ref=low.at[m],
             dst_ref=low.at[m],
-            send_sem=low_send.at[i],
-            recv_sem=low_recv.at[i],
+            send_sem=low_send.at[0],
+            recv_sem=low_recv.at[0],
             device_id={"mlp": lax.rem(m + i, 16)},
             device_id_type=MESH,
         )
@@ -436,11 +413,8 @@
     for h in range(2):
         in_product(h, 3)
 
-    def low_wait(i, c):
-        low_copy(i).wait()
-        return c
-
-    lax.fori_loop(1, 16, low_wait, 0)
+    wait_for(low.at[0:15], low_recv.at[0])
+    wait_for(low.at[0:15], low_send.at[0])
     lowrank = jnp.sum(low[...].astype(F32), axis=0).astype(BF16).astype(F32)
     for i in range(REQS):
         inside = (token >= starts[i]) & (token < ends[i])
@@ -452,8 +426,8 @@
         )
         preact = acc[i] + adapted.reshape(4, 32, UNITS)
         act[i] = jax.nn.gelu(preact, approximate=True).astype(BF16)
-    for copy in flying.values():
-        copy.wait_send()
+    for h in range(2):
+        wait_for(wo.at[0:240], ag_send.at[h])
 
     def nothing():
         return None
@@ -464,16 +438,8 @@
         cs = cols_of(h, "W")
         value = resid[:, cs] + (total[:, cs] + full2_f[h].astype(F32) + full2_b[h].astype(F32))
         outb[:, cs] = value.astype(BF16)
-    local(15, outb, out_hbm)
-
-    def a2a_sent(i, c):
-        for t, ref in enumerate((q_hbm, k_hbm, v_hbm)):
-            a2a_copy(t, ref, i).wait_send()
-        return c
-
-    lax.fori_loop(1, 16, a2a_sent, 0)
-    for i in (13, 14, 15):
-        locals_[i].wait()
+
+    wait_for(qkv.at[:, 0:480], a2a_send.at[0])
 
 
 def shards(*args):
@@ -515,28 +481,27 @@
         vmem((REQS * RANK, UNITS), BF16),
         vmem((16, RANK, TOK_G), BF16),
         vmem((REQS * RANK, TOK_G), BF16),
-        vmem((32, WIDTH), BF16),
-        dma((16,)),
-        dma((3, 16)),
-        dma((3, 16)),
-        dma((2, 8)),
-        dma((2, 8)),
-        dma((16,)),
-        dma((16,)),
-        dma((2, 28)),
-        dma((2, 28)),
-        dma((2, 20)),
-        dma((2, 20)),
+        dma((8,)),
+        dma((1,)),
+        dma((1,)),
+        dma((2,)),
+        dma((2,)),
+        dma((1,)),
+        dma((1,)),
+        dma((2,)),
+        dma((2, 15)),
+        dma((2,)),
+        dma((2, 15)),
     ]
     return pl.pallas_call(
         kernel,
         out_shape=(
-            jax.ShapeDtypeStruct((32, WIDTH), BF16),
-            jax.ShapeDtypeStruct((5, 128, HEADC), BF16),
-            jax.ShapeDtypeStruct((5, 128, HEADC), BF16),
+            pltpu.VMEM((32, WIDTH), BF16),
+            pltpu.VMEM((5, 128, HEADC), BF16),
+            pltpu.VMEM((5, 128, HEADC), BF16),
         ),
         in_specs=[any_] * 13 + [smem] * 4,
-        out_specs=(any_, any_, any_),
+        out_specs=(pl.BlockSpec(memory_space=pltpu.VMEM),) * 3,
         scratch_shapes=scratch,
         compiler_params=pltpu.CompilerParams(
             collective_id=0, has_side_effects=True, vmem_limit_bytes=62 * 1024 * 1024

time: 131 us -> 125 us (0.954)
  Pallas kernels: 125 us -> 121 us
  local copies, waits for them, and re-layouts: 5.15 us -> 2.17 us
    pallas_call x1, Pallas kernels: 125 us -> 121 us  [shards(): pl.pallas_call(kernel, out_shape=(pltpu.VMEM((32, WIDTH), BF16), pltpu.VM...]
    unnamed x3, local copies, waits for them, and re-layouts: 5.15 us -> 2.17 us
where the time goes in v2:
time: 125 us; the launch traced here: 124 us
  Pallas kernels  121 us (97%)
  local copies, waits for them, and re-layouts  2.17 us (2%)
    pallas_call x1, Pallas kernels, shards(): pl.pallas_call(kernel, out_shape=(pltpu.VMEM((32, WIDTH), BF16), pltpu.VM...  121 us

profile of v2, /device:TPU:0, one launch (start us, length us, event | category | flops | bytes accessed | tf_op | source)
XLA Modules:
  0.0 124.2 jit_solution(13249301195890792024)
XLA Ops:
  0.6 121.4 %shard_map.184 = (bf16[32,5120]{1,0:T(8,128)(2,1)S(1)}, bf16[5,128,256]{2,1,0:T(8,128)(2,1)S(1)}, bf16[5,128,256]{2,1,0:T(8,128)(2,1)S(1)}) custom-call(bf16[32,4096]{1,0:T(8,128)(2,1)} %q_hbm.1, bf16[32,4096]{1,0:T(8,128)(2,1)} %k_hbm.1, bf16[32,4096]{1,0:T(8,128)(2,1)} %v_hbm.1, bf16[32,5120]{1,0:T(8,128)(2,1)} %hid_hbm.1, bf16[256,5120]{1,0:T(8,128)(2,1)} %wo_hbm.1, ...), custom_call_target="tpu_custom_call" | custom-call | tf_op jit(solution)/shard_map/pallas_call | solution.py:496
  122.0 0.7 copy.23
  122.7 0.7 copy.24
  123.5 0.7 copy.25

commit v3 on v2

v3 whole, which is shorter than its diff:
```python
import functools

import jax
import jax.numpy as jnp
from jax import lax
from jax.experimental import pallas as pl
from jax.experimental.pallas import tpu as pltpu
from jax.sharding import PartitionSpec as P

MESH = pl.DeviceIdType.MESH
HS = 128
RANK = 16
REQS = 16
TOK_G = 512
WIDTH = 5120
HALF = WIDTH // 2
QUART = HALF // 2
UNITS = 864
HEADC = 256
TILE = 512
EPS = 1e-06
F32 = jnp.float32
BF16 = jnp.bfloat16

RELAY_F, RELAY_B, FULL = range(3)
R2F, R2B, FULL2 = range(12, 15)
OWN_F, OWN_B, REL = range(3)


def nt_dot(a, b):
    return lax.dot_general(a, b, (((1,), (1,)), ((), ())), preferred_element_type=F32)


def kernel(
    q_hbm, k_hbm, v_hbm, hid_hbm, wo_hbm, wi_hbm, w2_hbm, gain_hbm, bias_hbm, down_hbm, up_hbm, kc_hbm, vc_hbm,
    lens, look, adp, slot,
    outb, ko, vo,
    qkv, att, wo, wi, w2, hid, gain, bias, downs, ups, kc, vc, start_col,
    part, norm, relay_f, relay_b, full_f, full_b, mid, relay2_f, relay2_b, full2_f, full2_b,
    resid, total, acc, act, onehot, dsel_f, dsel, usel, low, spread,
    local_sem, a2a_send, a2a_recv, fac_send, fac_recv, low_send, low_recv, rs_send, rs_recv, ag_send, ag_recv,
):
    m = lax.axis_index("mlp")
    r = lax.axis_index("req")
    y, z = lax.div(m, 4), lax.rem(m, 4)

    def place(h, p, s):
        return (p, s) if h == 0 else (s, p)

    def device(h, p, s):
        a, b = place(h, p, s)
        return {"mlp": a * 4 + b}

    prim = (y, z)
    sec = (z, y)

    def up1(i, by):
        return lax.rem(i + by, 4)

    def wait_for(like, sem):
        pltpu.make_async_copy(like, like, sem).wait()

    locals_ = {}

    def local(i, src, dst):
        c = pltpu.make_async_copy(src, dst, local_sem.at[i])
        c.start()
        locals_[i] = c

    local(0, wo_hbm, wo)
    local(3, hid_hbm, hid)
    local(4, gain_hbm, gain)
    local(5, bias_hbm, bias)
    local(6, kc_hbm, kc)
    local(7, vc_hbm, vc)
    pltpu.make_async_copy(down_hbm, downs.at[r], fac_recv.at[0]).start()
    pltpu.make_async_copy(up_hbm, ups.at[r], fac_recv.at[1]).start()
    own_rows = pl.ds(pl.multiple_of(m * 32, 32), 32)
    for h in range(2):
        for t, ref in enumerate((q_hbm, k_hbm, v_hbm)):
            cols = pl.ds(pl.multiple_of(m * HEADC + h * HS, HS), HS)
            mine = qkv.at[t, own_rows, h * HS : (h + 1) * HS]
            pltpu.make_async_copy(ref.at[:, cols], mine, a2a_recv.at[h]).start()

    barrier = pltpu.get_barrier_semaphore()

    def greet_mlp(i, c):
        pl.semaphore_signal(barrier, inc=1, device_id={"mlp": lax.rem(m + i, 16)}, device_id_type=MESH)
        return c

    def greet_req(i, c):
        pl.semaphore_signal(barrier, inc=1, device_id={"req": lax.rem(r + i, 8)}, device_id_type=MESH)
        return c

    lax.fori_loop(1, 16, greet_mlp, 0)
    lax.fori_loop(1, 8, greet_req, 0)
    pl.semaphore_wait(barrier, 22)

    def a2a_copy(h, t, ref, i):
        d = lax.rem(m + i, 16)
        return pltpu.make_async_remote_copy(
            src_ref=ref.at[:, pl.ds(pl.multiple_of(d * HEADC + h * HS, HS), HS)],
            dst_ref=qkv.at[t, own_rows, h * HS : (h + 1) * HS],
            send_sem=a2a_send.at[0],
            recv_sem=a2a_recv.at[h],
            device_id={"mlp": d},
            device_id_type=MESH,
        )

    for h in range(2):

        def a2a_start(i, c, h=h):
            for t, ref in enumerate((q_hbm, k_hbm, v_hbm)):
                a2a_copy(h, t, ref, i).start()
            return c

        lax.fori_loop(1, 16, a2a_start, 0)

    def fac_copy(t, src, dst, i):
        return pltpu.make_async_remote_copy(
            src_ref=src,
            dst_ref=dst.at[r],
            send_sem=fac_send.at[t],
            recv_sem=fac_recv.at[t],
            device_id={"req": lax.rem(r + i, 8)},
            device_id_type=MESH,
        )

    def fac_start(i, c):
        fac_copy(0, down_hbm, downs, i).start()
        fac_copy(1, up_hbm, ups, i).start()
        return c

    lax.fori_loop(1, 8, fac_start, 0)
    local(1, wi_hbm, wi)
    local(2, w2_hbm, w2)

    pos = lax.broadcasted_iota(jnp.int32, (TOK_G, 1), 0)
    starts, ends = [], []
    first = jnp.zeros((TOK_G, 1), jnp.int32)
    end = jnp.int32(0)
    for i in range(REQS):
        starts.append(end)
        end = end + lens[0, i]
        ends.append(end)
        first = jnp.where(pos >= end, end, first)
    start_col[...] = first

    for i in range(REQS):
        wanted = slot[adp[0, i]] * RANK
        lane = lax.broadcasted_iota(jnp.int32, (RANK, 64 * RANK), 1)
        sub = lax.broadcasted_iota(jnp.int32, (RANK, 64 * RANK), 0)
        onehot[i * RANK : (i + 1) * RANK, :] = (lane - sub == wanted).astype(F32).astype(BF16)
    acc[...] = jnp.zeros_like(acc)


    for h in range(2):
        hc = slice(h * HS, (h + 1) * HS)
        wait_for(qkv.at[:, :, hc], a2a_recv.at[h])
        for i in range(4):
            rows, length = slice(i * 128, (i + 1) * 128), (i + 1) * 128
            score = nt_dot(qkv[0, rows, hc], qkv[1, :length, hc]) * (HS ** (-0.5))
            qi = lax.broadcasted_iota(jnp.int32, (128, length), 0) + i * 128
            kj = lax.broadcasted_iota(jnp.int32, (128, length), 1)
            allowed = (kj <= qi) & (kj >= start_col[rows, :])
            score = jnp.where(allowed, score, -1e30)
            expo = jnp.exp(score - jnp.max(score, axis=1, keepdims=True))
            weights = (expo / jnp.sum(expo, axis=1, keepdims=True)).astype(BF16)
            mixed = jnp.dot(weights, qkv[2, :length, hc], preferred_element_type=F32)
            att[i, :, :, hc] = mixed.astype(BF16).reshape(4, 32, HS)

    def remote(src, dst, sems, t, h, i, dev):
        c = pltpu.make_async_remote_copy(
            src_ref=src,
            dst_ref=dst,
            send_sem=sems[0].at[t, h],
            recv_sem=sems[1].at[t, h, i],
            device_id=dev,
            device_id_type=MESH,
        )
        c.start()

    def rows_of(t):
        return slice(16 * t, 16 * t + 16)

    def cols_of(h, which):
        base = h * HALF
        if which == "F":
            return slice(base, base + QUART)
        if which == "B":
            return slice(base + QUART, base + HALF)
        return slice(base, base + HALF)

    UNIT, PIECE, PAIR, SENT = wo.at[0:16, :QUART], wo.at[0:16, :HALF], wo.at[0:16], wo.at[0:240, :HALF]

    class Scatter:
        def __init__(self, t, left, right):
            self.t, self.left, self.right = t, left, right
            self.sems = (rs_send, rs_recv)

        def at(self, h, p, s, which):
            a, b = place(h, p, s)
            return (a, b, rows_of(self.t), cols_of(h, which))

        def order(self, h, k):
            return up1(sec[h], (2, 1, 3, 0)[k])

        def product(self, h, k):
            s, rows = self.order(h, k), rows_of(self.t)
            left, right = self.left, self.right
            lhs = left[:, s, rows] if h == 0 else left[s, :, rows]
            lhs = lhs.reshape(64, left.shape[3])
            for c in range(h * HALF, (h + 1) * HALF, TILE):
                value = jnp.dot(lhs, right[:, c : c + TILE], preferred_element_type=F32).astype(BF16)
                value = value.reshape(4, 16, TILE)
                if h == 0:
                    part[:, s, rows, c : c + TILE] = value
                else:
                    part[s, :, rows, c : c + TILE] = value

        def first(self, k):
            t, rows, sems = self.t, rows_of(self.t), self.sems
            for h in range(2):
                self.product(h, k)
                p, s, sp = prim[h], sec[h], self.order(h, k)
                ahead, behind = device(h, up1(p, 1), s), device(h, up1(p, 3), s)
                far, i = up1(p, 2), 3 * k
                remote(part.at[self.at(h, far, sp, "F")], relay_f.at[h, k, rows], sems, t, h, i + RELAY_F, ahead)
                remote(part.at[self.at(h, far, sp, "B")], relay_b.at[h, k, rows], sems, t, h, i + RELAY_B, behind)
                remote(part.at[self.at(h, up1(p, 1), sp, "B")], full_f.at[h, k, rows, QUART:], sems, t, h, i + FULL, ahead)
                remote(part.at[self.at(h, up1(p, 3), sp, "F")], full_b.at[h, k, rows, :QUART], sems, t, h, i + FULL, behind)

        def second(self, k):
            t, rows, sems = self.t, rows_of(self.t), self.sems
            for h in range(2):
                p, s, sp = prim[h], sec[h], self.order(h, k)
                ahead, behind = device(h, up1(p, 1), s), device(h, up1(p, 3), s)
                i = 3 * k
                wait_for(UNIT, rs_recv.at[t, h, i + RELAY_F])
                at = self.at(h, up1(p, 1), sp, "F")
                part[at] = (part[at].astype(F32) + relay_f[h, k, rows].astype(F32)).astype(BF16)
                remote(part.at[at], full_f.at[h, k, rows, :QUART], sems, t, h, i + FULL, ahead)
                wait_for(UNIT, rs_recv.at[t, h, i + RELAY_B])
                at = self.at(h, up1(p, 3), sp, "B")
                part[at] = (part[at].astype(F32) + relay_b[h, k, rows].astype(F32)).astype(BF16)
                remote(part.at[at], full_b.at[h, k, rows, QUART:], sems, t, h, i + FULL, behind)

        def third(self, k):
            t, rows, sems = self.t, rows_of(self.t), self.sems
            for h in range(2):
                p, s, sp = prim[h], sec[h], self.order(h, k)
                wait_for(PAIR, rs_recv.at[t, h, 3 * k + FULL])
                value = (
                    part[self.at(h, p, sp, "W")].astype(F32)
                    + full_f[h, k, rows].astype(F32)
                    + full_b[h, k, rows].astype(F32)
                )
                ahead, behind = device(h, p, up1(s, 1)), device(h, p, up1(s, 3))
                if k == 0:
                    mid[h, 0, rows] = value.astype(BF16)
                    remote(mid.at[h, 0, rows, :QUART], relay2_f.at[h, rows], sems, t, h, R2F, ahead)
                    remote(mid.at[h, 0, rows, QUART:], relay2_b.at[h, rows], sems, t, h, R2B, behind)
                elif k == 1:
                    wait_for(UNIT, rs_recv.at[t, h, R2F])
                    mid[h, 1, rows, :QUART] = (value[:, :QUART] + relay2_f[h, rows].astype(F32)).astype(BF16)
                    mid[h, 1, rows, QUART:] = value[:, QUART:].astype(BF16)
                    remote(mid.at[h, 1, rows], full2_f.at[h, rows], sems, t, h, FULL2, ahead)
                elif k == 2:
                    wait_for(UNIT, rs_recv.at[t, h, R2B])
                    mid[h, 2, rows, :QUART] = value[:, :QUART].astype(BF16)
                    mid[h, 2, rows, QUART:] = (value[:, QUART:] + relay2_b[h, rows].astype(F32)).astype(BF16)
                    remote(mid.at[h, 2, rows], full2_b.at[h, rows], sems, t, h, FULL2, behind)
                else:
                    total[rows, cols_of(h, "W")] = value

        def last(self):
            rows = rows_of(self.t)
            for h in range(2):
                wait_for(PAIR, rs_recv.at[self.t, h, FULL2])
                wait_for(SENT, rs_send.at[self.t, h])
            return [
                total[rows, cols_of(h, "W")] + full2_f[h, rows].astype(F32) + full2_b[h, rows].astype(F32)
                for h in range(2)
            ]

    class Gather:
        def __init__(self, t):
            self.t = t
            self.sems = (ag_send, ag_recv)

        def order(self, h, k):
            return up1(sec[h], (0, 3, 1, 2)[k])

        def put(self, h, i, pp, sp, which, dev):
            a, b = place(h, pp, sp)
            ref = norm.at[a, b, rows_of(self.t), cols_of(h, which)]
            remote(ref, ref, self.sems, self.t, h, i, dev)

        def one(self, h, i, sp, which, by):
            self.put(h, i, prim[h], sp, which, device(h, prim[h], up1(sec[h], by)))

        def two(self, h, k, i, pp, which, by):
            self.put(h, 3 + 3 * k + i, pp, self.order(h, k), which, device(h, up1(prim[h], by), sec[h]))

        def own(self, h, k):
            self.two(h, k, OWN_F, prim[h], "W", 1)
            self.two(h, k, OWN_B, prim[h], "W", 3)

        def wait(self, h, i):
            wait_for(PIECE, ag_recv.at[self.t, h, i])

        def norms(self, sums):
            rows = rows_of(self.t)
            for h in range(2):
                cs = cols_of(h, "W")
                resid[rows, cs] = hid[rows, cs].astype(F32) + sums[h]
            mean = jnp.sum(resid[rows], axis=1, keepdims=True) * (1.0 / WIDTH)
            centered = resid[rows] - mean
            var = jnp.sum(centered * centered, axis=1, keepdims=True) * (1.0 / WIDTH)
            norm[y, z, rows] = (centered * lax.rsqrt(var + EPS) * gain[...] + bias[...]).astype(BF16)

        def start(self):
            for h in range(2):
                self.one(h, OWN_F, sec[h], "W", 1)
                self.one(h, OWN_B, sec[h], "W", 3)
            for h in range(2):
                self.own(h, 0)

        def near(self):
            for h in range(2):
                self.wait(h, OWN_F)
                self.one(h, REL, up1(sec[h], 3), "F", 1)
                self.own(h, 1)
                self.wait(h, OWN_B)
                self.one(h, REL, up1(sec[h], 1), "B", 3)
                self.own(h, 2)

        def far(self):
            for h in range(2):
                self.wait(h, REL)
                self.own(h, 3)

        def relay(self, k):
            for h in range(2):
                self.wait(h, 3 + 3 * k + OWN_F)
                self.two(h, k, REL, up1(prim[h], 3), "F", 1)
                self.wait(h, 3 + 3 * k + OWN_B)
                self.two(h, k, REL, up1(prim[h], 1), "B", 3)

        def done(self, k):
            for h in range(2):
                self.wait(h, 3 + 3 * k + REL)

        def product(self, k):
            rows = rows_of(self.t)
            for h in range(2):
                sp, cs = self.order(h, k), cols_of(h, "W")
                lhs = norm[:, sp, rows, cs] if h == 0 else norm[sp, :, rows, cs]
                value = nt_dot(lhs.reshape(64, HALF), wi[:, cs]).reshape(4, 16, UNITS)
                if h == 0:
                    acc[:, sp, rows] = acc[:, sp, rows] + value
                else:
                    acc[sp, :, rows] = acc[sp, :, rows] + value

        def low_copy(self, i):
            ref = low.at[self.t, m]
            return pltpu.make_async_remote_copy(
                src_ref=ref,
                dst_ref=ref,
                send_sem=low_send.at[self.t],
                recv_sem=low_recv.at[self.t],
                device_id={"mlp": lax.rem(m + i, 16)},
                device_id_type=MESH,
            )

        def inside(self, i):
            lane = lax.broadcasted_iota(jnp.int32, (RANK, 256), 1)
            token = (lane >> 4) * 32 + (lane & 15) + 16 * self.t
            return (token >= starts[i]) & (token < ends[i])

        def lows(self):
            window = pl.ds(pl.multiple_of(lax.div(m * 5 - lax.rem(m, 2), 2) * 128, 128), 384)
            ranks = nt_dot(dsel[...], norm[:, :, rows_of(self.t), window].reshape(256, 384))
            mine = jnp.zeros((RANK, 256), F32)
            for i in range(REQS):
                mine = mine + jnp.where(self.inside(i), ranks[i * RANK : (i + 1) * RANK, :], 0.0)
            low[self.t, m] = mine.astype(BF16)

            def low_start(i, c):
                self.low_copy(i).start()
                return c

            lax.fori_loop(1, 16, low_start, 0)

        def activate(self):
            t, rows = self.t, rows_of(self.t)
            wait_for(low.at[t, 0:15], low_recv.at[t])
            wait_for(low.at[t, 0:15], low_send.at[t])
            lowrank = jnp.sum(low[t].astype(F32), axis=0).astype(BF16).astype(F32)
            for i in range(REQS):
                spread[i * RANK : (i + 1) * RANK, :] = jnp.where(self.inside(i), lowrank, 0.0).astype(BF16)
            for i in range(2):
                adapted = lax.dot_general(
                    spread[:, i * 128 : (i + 1) * 128], usel[...], (((0,), (0,)), ((), ())), preferred_element_type=F32
                )
                two = slice(2 * i, 2 * i + 2)
                preact = acc[two, :, rows] + adapted.reshape(2, 4, 16, UNITS)
                act[two, :, rows] = jax.nn.gelu(preact, approximate=True).astype(BF16)
            for h in range(2):
                wait_for(SENT, ag_send.at[t, h])

    def pages():
        locals_[6].wait()
        locals_[7].wait()
        for t, cache, out in ((1, kc, ko), (2, vc, vo)):
            for page in range(5):
                value = cache[page]
                for b in range(4):
                    value = jnp.where(look[0, b] == page, qkv[t, b * 128 : (b + 1) * 128, :], value)
                out[page] = value

    def pick_down():
        for t, ref in enumerate((downs, ups)):
            wait_for(ref, fac_recv.at[t])
            wait_for(ref.at[0:7], fac_send.at[t])
        picked = jnp.dot(onehot[...], downs[...].reshape(64 * RANK, 320), preferred_element_type=F32)
        dsel_f[...] = jnp.zeros_like(dsel_f)
        dsel_f[:, :320] = picked
        shifted = jnp.where(lax.rem(m, 2) == 1, pltpu.roll(dsel_f[...], 64, 1), dsel_f[...])
        dsel[...] = shifted.astype(BF16)

    def pick_up():
        usel[...] = jnp.dot(onehot[...], ups[...].reshape(64 * RANK, UNITS), preferred_element_type=F32).astype(BF16)

    locals_[0].wait()
    locals_[3].wait()
    a, b = Scatter(0, att, wo), Scatter(1, att, wo)
    c, d = Scatter(0, act, w2), Scatter(1, act, w2)
    ga, gb = Gather(0), Gather(1)
    a.first(0)
    a.first(1)
    b.first(0)
    a.second(0)
    b.first(1)
    a.first(2)
    a.first(3)
    b.second(0)
    a.third(0)
    a.second(1)
    a.second(2)
    b.first(2)
    a.second(3)
    a.third(1)
    a.third(2)
    b.third(0)
    b.second(1)
    b.first(3)
    a.third(3)
    locals_[4].wait()
    locals_[5].wait()
    ga.norms(a.last())
    ga.start()
    b.second(2)
    ga.near()
    b.third(1)
    b.third(2)
    b.second(3)
    ga.far()
    ga.relay(2)
    ga.relay(0)
    pick_down()
    ga.relay(1)
    pick_up()
    b.third(3)
    ga.relay(3)
    gb.norms(b.last())
    gb.start()
    ga.done(2)
    pages()
    ga.done(0)
    locals_[1].wait()
    ga.product(2)
    ga.done(3)
    ga.done(1)
    ga.lows()
    ga.product(3)
    gb.near()
    ga.product(0)
    gb.relay(0)
    ga.product(1)
    ga.activate()
    gb.far()
    locals_[2].wait()
    c.first(0)
    gb.relay(1)
    gb.relay(2)
    gb.done(0)
    gb.product(0)
    gb.relay(3)
    c.first(1)
    c.first(2)
    gb.done(1)
    c.second(0)
    gb.product(1)
    gb.done(2)
    gb.done(3)
    gb.lows()
    c.second(1)
    c.first(3)
    gb.product(3)
    gb.product(2)
    c.third(0)
    c.second(2)
    c.second(3)
    gb.activate()
    d.first(0)
    d.first(1)
    d.first(2)
    d.second(0)
    d.second(1)
    d.first(3)
    d.third(0)
    d.second(2)
    d.second(3)
    c.third(1)
    c.third(2)
    d.third(1)
    c.third(3)
    d.third(2)
    sums = c.last()
    for h in range(2):
        outb[0:16, cols_of(h, "W")] = (resid[0:16, cols_of(h, "W")] + sums[h]).astype(BF16)
    d.third(3)
    sums = d.last()
    for h in range(2):
        outb[16:32, cols_of(h, "W")] = (resid[16:32, cols_of(h, "W")] + sums[h]).astype(BF16)
    wait_for(qkv.at[:, 0:480], a2a_send.at[0])


def shards(*args):
    (queries, keys, values, hidden, w_o, w_in, w_out, gain, bias, down, up, kc, vc, lens, look, adp, slot) = args
    any_, smem = pl.BlockSpec(memory_space=pl.ANY), pl.BlockSpec(memory_space=pltpu.SMEM)
    vmem, dma = pltpu.VMEM, pltpu.SemaphoreType.DMA
    scratch = [
        vmem((3, TOK_G, HEADC), BF16),
        vmem((4, 4, 32, HEADC), BF16),
        vmem((HEADC, WIDTH), BF16),
        vmem((UNITS, WIDTH), BF16),
        vmem((UNITS, WIDTH), BF16),
        vmem((32, WIDTH), BF16),
        vmem((1, WIDTH), F32),
        vmem((1, WIDTH), F32),
        vmem((8, 128, 320), BF16),
        vmem((8, 128, UNITS), BF16),
        vmem((5, 128, HEADC), BF16),
        vmem((5, 128, HEADC), BF16),
        vmem((TOK_G, 1), jnp.int32),
        vmem((4, 4, 32, WIDTH), BF16),
        vmem((4, 4, 32, WIDTH), BF16),
        vmem((2, 4, 32, QUART), BF16),
        vmem((2, 4, 32, QUART), BF16),
        vmem((2, 4, 32, HALF), BF16),
        vmem((2, 4, 32, HALF), BF16),
        vmem((2, 3, 32, HALF), BF16),
        vmem((2, 32, QUART), BF16),
        vmem((2, 32, QUART), BF16),
        vmem((2, 32, HALF), BF16),
        vmem((2, 32, HALF), BF16),
        vmem((32, WIDTH), F32),
        vmem((32, WIDTH), F32),
        vmem((4, 4, 32, UNITS), F32),
        vmem((4, 4, 32, UNITS), BF16),
        vmem((REQS * RANK, 64 * RANK), BF16),
        vmem((REQS * RANK, 384), F32),
        vmem((REQS * RANK, 384), BF16),
        vmem((REQS * RANK, UNITS), BF16),
        vmem((2, 16, RANK, 256), BF16),
        vmem((REQS * RANK, 256), BF16),
        dma((8,)),
        dma((1,)),
        dma((2,)),
        dma((2,)),
        dma((2,)),
        dma((2,)),
        dma((2,)),
        dma((2, 2)),
        dma((2, 2, 15)),
        dma((2, 2)),
        dma((2, 2, 15)),
    ]
    return pl.pallas_call(
        kernel,
        out_shape=(
            pltpu.VMEM((32, WIDTH), BF16),
            pltpu.VMEM((5, 128, HEADC), BF16),
            pltpu.VMEM((5, 128, HEADC), BF16),
        ),
        in_specs=[any_] * 13 + [smem] * 4,
        out_specs=(pl.BlockSpec(memory_space=pltpu.VMEM),) * 3,
        scratch_shapes=scratch,
        compiler_params=pltpu.CompilerParams(
            collective_id=0, has_side_effects=True, vmem_limit_bytes=62 * 1024 * 1024
        ),
    )(
        queries, keys, values, hidden, w_o, w_in.T, w_out, gain.reshape(1, WIDTH), bias.reshape(1, WIDTH),
        jnp.transpose(down, (0, 2, 1)).reshape(128, 320), up.reshape(128, UNITS), kc, vc, lens, look, adp, slot,
    )


def solution(mesh):
    in_specs = (
        P(("req", "mlp"), None),
        P(("req", "mlp"), None),
        P(("req", "mlp"), None),
        P(("req", "mlp"), None),
        P("mlp", None),
        P(None, "mlp"),
        P("mlp", None),
        P(),
        P(),
        P("req", "mlp", None),
        P("req", None, "mlp"),
        P("req", None, "mlp"),
        P("req", None, "mlp"),
        P("req", None),
        P("req", None),
        P("req", None),
        P(),
    )
    out_specs = (P(("req", "mlp"), None), P("req", None, "mlp"), P("req", None, "mlp"))
    return jax.shard_map(shards, mesh=mesh, in_specs=in_specs, out_specs=out_specs, check_vma=False)
```

time: 125 us -> 119 us (0.952)
  Pallas kernels: 121 us -> 116 us
    pallas_call x1, Pallas kernels: 121 us -> 116 us  [shards(): pl.pallas_call(kernel, out_shape=(pltpu.VMEM((32, WIDTH), BF16), pltpu.VM...]
where the time goes in v3:
time: 119 us
  Pallas kernels  116 us (97%)
  local copies, waits for them, and re-layouts  2.17 us (2%)
    pallas_call x1, Pallas kernels, shards(): pl.pallas_call(kernel, out_shape=(pltpu.VMEM((32, WIDTH), BF16), pltpu.VM...  116 us

profile of v3, /device:TPU:0, one launch (start us, length us, event | category | flops | bytes accessed | tf_op | source)
XLA Modules:
  0.0 118.7 jit_solution(5317234744067985708)
XLA Ops:
  0.6 115.9 %shard_map.184 = (bf16[32,5120]{1,0:T(8,128)(2,1)S(1)}, bf16[5,128,256]{2,1,0:T(8,128)(2,1)S(1)}, bf16[5,128,256]{2,1,0:T(8,128)(2,1)S(1)}) custom-call(bf16[32,4096]{1,0:T(8,128)(2,1)} %q_hbm.1, bf16[32,4096]{1,0:T(8,128)(2,1)} %k_hbm.1, bf16[32,4096]{1,0:T(8,128)(2,1)} %v_hbm.1, bf16[32,5120]{1,0:T(8,128)(2,1)} %hid_hbm.1, bf16[256,5120]{1,0:T(8,128)(2,1)} %wo_hbm.1, ...), custom_call_target="tpu_custom_call" | custom-call | tf_op jit(solution)/shard_map/pallas_call | solution.py:591
  116.5 0.7 copy.23
  117.3 0.7 copy.24
  118.0 0.7 copy.25

commit v4 on v3

--- a/solution.py
+++ b/solution.py
@@ -22,9 +22,9 @@
 F32 = jnp.float32
 BF16 = jnp.bfloat16
 
-RELAY_F, RELAY_B, FULL = range(3)
-R2F, R2B, FULL2 = range(12, 15)
-OWN_F, OWN_B, REL = range(3)
+RELAY, FULL = range(2)
+R2F, R2B, FULL2 = range(8, 11)
+OWN, REL = range(2)
 
 
 def nt_dot(a, b):
@@ -218,29 +218,27 @@
                 else:
                     part[s, :, rows, c : c + TILE] = value
 
-        def first(self, k):
+        def first(self, k, h):
             t, rows, sems = self.t, rows_of(self.t), self.sems
-            for h in range(2):
-                self.product(h, k)
+            self.product(h, k)
+            p, s, sp = prim[h], sec[h], self.order(h, k)
+            ahead, behind = device(h, up1(p, 1), s), device(h, up1(p, 3), s)
+            far, i = up1(p, 2), 2 * k
+            remote(part.at[self.at(h, far, sp, "F")], relay_f.at[h, k, rows], sems, t, h, i + RELAY, ahead)
+            remote(part.at[self.at(h, far, sp, "B")], relay_b.at[h, k, rows], sems, t, h, i + RELAY, behind)
+            remote(part.at[self.at(h, up1(p, 1), sp, "B")], full_f.at[h, k, rows, QUART:], sems, t, h, i + FULL, ahead)
+            remote(part.at[self.at(h, up1(p, 3), sp, "F")], full_b.at[h, k, rows, :QUART], sems, t, h, i + FULL, behind)
+
+        def second(self, k):
+            t, rows, sems = self.t, rows_of(self.t), self.sems
+            for h in range(2):
                 p, s, sp = prim[h], sec[h], self.order(h, k)
                 ahead, behind = device(h, up1(p, 1), s), device(h, up1(p, 3), s)
-                far, i = up1(p, 2), 3 * k
-                remote(part.at[self.at(h, far, sp, "F")], relay_f.at[h, k, rows], sems, t, h, i + RELAY_F, ahead)
-                remote(part.at[self.at(h, far, sp, "B")], relay_b.at[h, k, rows], sems, t, h, i + RELAY_B, behind)
-                remote(part.at[self.at(h, up1(p, 1), sp, "B")], full_f.at[h, k, rows, QUART:], sems, t, h, i + FULL, ahead)
-                remote(part.at[self.at(h, up1(p, 3), sp, "F")], full_b.at[h, k, rows, :QUART], sems, t, h, i + FULL, behind)
-
-        def second(self, k):
-            t, rows, sems = self.t, rows_of(self.t), self.sems
-            for h in range(2):
-                p, s, sp = prim[h], sec[h], self.order(h, k)
-                ahead, behind = device(h, up1(p, 1), s), device(h, up1(p, 3), s)
-                i = 3 * k
-                wait_for(UNIT, rs_recv.at[t, h, i + RELAY_F])
+                i = 2 * k
+                wait_for(PIECE, rs_recv.at[t, h, i + RELAY])
                 at = self.at(h, up1(p, 1), sp, "F")
                 part[at] = (part[at].astype(F32) + relay_f[h, k, rows].astype(F32)).astype(BF16)
                 remote(part.at[at], full_f.at[h, k, rows, :QUART], sems, t, h, i + FULL, ahead)
-                wait_for(UNIT, rs_recv.at[t, h, i + RELAY_B])
                 at = self.at(h, up1(p, 3), sp, "B")
                 part[at] = (part[at].astype(F32) + relay_b[h, k, rows].astype(F32)).astype(BF16)
                 remote(part.at[at], full_b.at[h, k, rows, QUART:], sems, t, h, i + FULL, behind)
@@ -249,7 +247,7 @@
             t, rows, sems = self.t, rows_of(self.t), self.sems
             for h in range(2):
                 p, s, sp = prim[h], sec[h], self.order(h, k)
-                wait_for(PAIR, rs_recv.at[t, h, 3 * k + FULL])
+                wait_for(PAIR, rs_recv.at[t, h, 2 * k + FULL])
                 value = (
                     part[self.at(h, p, sp, "W")].astype(F32)
                     + full_f[h, k, rows].astype(F32)
@@ -300,14 +298,14 @@
             self.put(h, i, prim[h], sp, which, device(h, prim[h], up1(sec[h], by)))
 
         def two(self, h, k, i, pp, which, by):
-            self.put(h, 3 + 3 * k + i, pp, self.order(h, k), which, device(h, up1(prim[h], by), sec[h]))
+            self.put(h, 2 + 2 * k + i, pp, self.order(h, k), which, device(h, up1(prim[h], by), sec[h]))
 
         def own(self, h, k):
-            self.two(h, k, OWN_F, prim[h], "W", 1)
-            self.two(h, k, OWN_B, prim[h], "W", 3)
+            self.two(h, k, OWN, prim[h], "W", 1)
+            self.two(h, k, OWN, prim[h], "W", 3)
 
         def wait(self, h, i):
-            wait_for(PIECE, ag_recv.at[self.t, h, i])
+            wait_for(PAIR if i % 2 == OWN else PIECE, ag_recv.at[self.t, h, i])
 
         def norms(self, sums):
             rows = rows_of(self.t)
@@ -321,17 +319,16 @@
 
         def start(self):
             for h in range(2):
-                self.one(h, OWN_F, sec[h], "W", 1)
-                self.one(h, OWN_B, sec[h], "W", 3)
+                self.one(h, OWN, sec[h], "W", 1)
+                self.one(h, OWN, sec[h], "W", 3)
             for h in range(2):
                 self.own(h, 0)
 
         def near(self):
             for h in range(2):
-                self.wait(h, OWN_F)
+                self.wait(h, OWN)
                 self.one(h, REL, up1(sec[h], 3), "F", 1)
                 self.own(h, 1)
-                self.wait(h, OWN_B)
                 self.one(h, REL, up1(sec[h], 1), "B", 3)
                 self.own(h, 2)
 
@@ -342,25 +339,23 @@
 
         def relay(self, k):
             for h in range(2):
-                self.wait(h, 3 + 3 * k + OWN_F)
+                self.wait(h, 2 + 2 * k + OWN)
                 self.two(h, k, REL, up1(prim[h], 3), "F", 1)
-                self.wait(h, 3 + 3 * k + OWN_B)
                 self.two(h, k, REL, up1(prim[h], 1), "B", 3)
 
         def done(self, k):
             for h in range(2):
-                self.wait(h, 3 + 3 * k + REL)
-
-        def product(self, k):
+                self.wait(h, 2 + 2 * k + REL)
+
+        def product(self, k, h):
             rows = rows_of(self.t)
-            for h in range(2):
-                sp, cs = self.order(h, k), cols_of(h, "W")
-                lhs = norm[:, sp, rows, cs] if h == 0 else norm[sp, :, rows, cs]
-                value = nt_dot(lhs.reshape(64, HALF), wi[:, cs]).reshape(4, 16, UNITS)
-                if h == 0:
-                    acc[:, sp, rows] = acc[:, sp, rows] + value
-                else:
-                    acc[sp, :, rows] = acc[sp, :, rows] + value
+            sp, cs = self.order(h, k), cols_of(h, "W")
+            lhs = norm[:, sp, rows, cs] if h == 0 else norm[sp, :, rows, cs]
+            value = nt_dot(lhs.reshape(64, HALF), wi[:, cs]).reshape(4, 16, UNITS)
+            if h == 0:
+                acc[:, sp, rows] = acc[:, sp, rows] + value
+            else:
+                acc[sp, :, rows] = acc[sp, :, rows] + value
 
         def low_copy(self, i):
             ref = low.at[self.t, m]
@@ -437,24 +432,32 @@
     a, b = Scatter(0, att, wo), Scatter(1, att, wo)
     c, d = Scatter(0, act, w2), Scatter(1, act, w2)
     ga, gb = Gather(0), Gather(1)
-    a.first(0)
-    a.first(1)
-    b.first(0)
+    a.first(0, 0)
+    a.first(0, 1)
+    a.first(1, 0)
+    a.first(1, 1)
+    b.first(0, 0)
+    b.first(0, 1)
     a.second(0)
-    b.first(1)
-    a.first(2)
-    a.first(3)
+    b.first(1, 0)
+    b.first(1, 1)
+    a.first(2, 0)
+    a.first(2, 1)
+    a.first(3, 0)
+    a.first(3, 1)
     b.second(0)
     a.third(0)
     a.second(1)
     a.second(2)
-    b.first(2)
+    b.first(2, 0)
+    b.first(2, 1)
     a.second(3)
     a.third(1)
     a.third(2)
     b.third(0)
     b.second(1)
-    b.first(3)
+    b.first(3, 0)
+    b.first(3, 1)
     a.third(3)
     locals_[4].wait()
     locals_[5].wait()
@@ -479,46 +482,62 @@
     pages()
     ga.done(0)
     locals_[1].wait()
-    ga.product(2)
+    ga.product(2, 0)
+    ga.product(2, 1)
     ga.done(3)
     ga.done(1)
     ga.lows()
-    ga.product(3)
+    ga.product(3, 0)
+    ga.product(3, 1)
     gb.near()
-    ga.product(0)
+    ga.product(0, 0)
+    ga.product(0, 1)
     gb.relay(0)
-    ga.product(1)
+    ga.product(1, 0)
+    ga.product(1, 1)
     ga.activate()
     gb.far()
     locals_[2].wait()
-    c.first(0)
+    c.first(0, 0)
+    c.first(0, 1)
     gb.relay(1)
     gb.relay(2)
     gb.done(0)
-    gb.product(0)
+    gb.product(0, 0)
+    gb.product(0, 1)
     gb.relay(3)
-    c.first(1)
-    c.first(2)
+    c.first(1, 0)
+    c.first(1, 1)
+    c.first(2, 0)
+    c.first(2, 1)
     gb.done(1)
     c.second(0)
-    gb.product(1)
+    gb.product(1, 0)
+    gb.product(1, 1)
     gb.done(2)
     gb.done(3)
     gb.lows()
     c.second(1)
-    c.first(3)
-    gb.product(3)
-    gb.product(2)
+    c.first(3, 0)
+    c.first(3, 1)
+    gb.product(3, 0)
+    gb.product(3, 1)
+    gb.product(2, 0)
+    gb.product(2, 1)
     c.third(0)
     c.second(2)
     c.second(3)
     gb.activate()
-    d.first(0)
-    d.first(1)
-    d.first(2)
+    d.first(0, 0)
+    d.first(0, 1)
+    d.first(1, 0)
+    d.first(1, 1)
+    d.first(2, 0)
+    d.first(2, 1)
     d.second(0)
     d.second(1)
-    d.first(3)
+    d.first(3, 0)
+    d.first(3, 1)
     d.third(0)
     d.second(2)
     d.second(3)
@@ -535,6 +554,25 @@
     for h in range(2):
         outb[16:32, cols_of(h, "W")] = (resid[16:32, cols_of(h, "W")] + sums[h]).astype(BF16)
     wait_for(qkv.at[:, 0:480], a2a_send.at[0])
+
+
+def writer(a, b, c, to_a, to_b, to_c, sem):
+    copies = [pltpu.make_async_copy(x, o, sem.at[i]) for i, (x, o) in enumerate(((a, to_a), (b, to_b), (c, to_c)))]
+    for copy in copies:
+        copy.start()
+    for copy in copies:
+        copy.wait()
+
+
+def written(results):
+    any_ = pl.BlockSpec(memory_space=pl.ANY)
+    return pl.pallas_call(
+        writer,
+        out_shape=tuple(jax.ShapeDtypeStruct(v.shape, v.dtype) for v in results),
+        in_specs=[pl.BlockSpec(memory_space=pltpu.VMEM)] * 3,
+        out_specs=(any_,) * 3,
+        scratch_shapes=[pltpu.SemaphoreType.DMA((3,))],
+    )(*(pltpu.with_memory_space_constraint(v, pltpu.VMEM) for v in results))
 
 
 def shards(*args):
@@ -584,11 +622,11 @@
         dma((2,)),
         dma((2,)),
         dma((2, 2)),
-        dma((2, 2, 15)),
+        dma((2, 2, 11)),
         dma((2, 2)),
-        dma((2, 2, 15)),
+        dma((2, 2, 10)),
     ]
-    return pl.pallas_call(
+    results = pl.pallas_call(
         kernel,
         out_shape=(
             pltpu.VMEM((32, WIDTH), BF16),
@@ -605,6 +643,7 @@
         queries, keys, values, hidden, w_o, w_in.T, w_out, gain.reshape(1, WIDTH), bias.reshape(1, WIDTH),
         jnp.transpose(down, (0, 2, 1)).reshape(128, 320), up.reshape(128, UNITS), kc, vc, lens, look, adp, slot,
     )
+    return written(results)
 
 
 def solution(mesh):

time: 119 us -> 118 us (level)
  local copies, waits for them, and re-layouts: 2.17 us -> 0 us
    unnamed x3 -> x0, local copies, waits for them, and re-layouts: 2.17 us -> none
where the time goes in v4:
time: 118 us
  Pallas kernels  117 us (99%)
    pallas_call x1, Pallas kernels, shards(): pl.pallas_call(kernel, out_shape=(pltpu.VMEM((32, WIDTH), BF16), pltpu.VM...  116 us

profile of v4, /device:TPU:0, one launch (start us, length us, event | category | flops | bytes accessed | tf_op | source)
XLA Modules:
  0.0 117.7 jit_solution(9245195546375793172)
XLA Ops:
  0.6 115.9 %shard_map.184 = (bf16[32,5120]{1,0:T(8,128)(2,1)S(1)}, bf16[5,128,256]{2,1,0:T(8,128)(2,1)S(1)}, bf16[5,128,256]{2,1,0:T(8,128)(2,1)S(1)}) custom-call(bf16[32,4096]{1,0:T(8,128)(2,1)} %q_hbm.1, bf16[32,4096]{1,0:T(8,128)(2,1)} %k_hbm.1, bf16[32,4096]{1,0:T(8,128)(2,1)} %v_hbm.1, bf16[32,5120]{1,0:T(8,128)(2,1)} %hid_hbm.1, bf16[256,5120]{1,0:T(8,128)(2,1)} %wo_hbm.1, ...), custom_call_target="tpu_custom_call" | custom-call | tf_op jit(solution)/shard_map/pallas_call | solution.py:629
  116.6 1.0 shard_map.185

commit v5 on v4

--- a/solution.py
+++ b/solution.py
@@ -96,8 +96,11 @@
     lax.fori_loop(1, 8, greet_req, 0)
     pl.semaphore_wait(barrier, 22)
 
+    def far_first(i):
+        return lax.rem(2 + 3 * i + 3 * lax.div(i * (i - 1), 2), 4)
+
     def a2a_copy(h, t, ref, i):
-        d = lax.rem(m + i, 16)
+        d = up1(y, far_first(lax.div(i, 4))) * 4 + up1(z, far_first(lax.rem(i, 4)))
         return pltpu.make_async_remote_copy(
             src_ref=ref.at[:, pl.ds(pl.multiple_of(d * HEADC + h * HS, HS), HS)],
             dst_ref=qkv.at[t, own_rows, h * HS : (h + 1) * HS],
@@ -114,7 +117,7 @@
                 a2a_copy(h, t, ref, i).start()
             return c
 
-        lax.fori_loop(1, 16, a2a_start, 0)
+        lax.fori_loop(0, 15, a2a_start, 0)
 
     def fac_copy(t, src, dst, i):
         return pltpu.make_async_remote_copy(

time: 118 us -> 117 us (level)
  no operation moved by 1% of the time
where the time goes in v5:
time: 117 us
  Pallas kernels  116 us (99%)
    pallas_call x1, Pallas kernels, shards(): pl.pallas_call(kernel, out_shape=(pltpu.VMEM((32, WIDTH), BF16), pltpu.VM...  115 us

profile of v5, /device:TPU:0, one launch (start us, length us, event | category | flops | bytes accessed | tf_op | source)
XLA Modules:
  0.0 117.2 jit_solution(5064237812799411214)
XLA Ops:
  0.6 115.4 %shard_map.184 = (bf16[32,5120]{1,0:T(8,128)(2,1)S(1)}, bf16[5,128,256]{2,1,0:T(8,128)(2,1)S(1)}, bf16[5,128,256]{2,1,0:T(8,128)(2,1)S(1)}) custom-call(bf16[32,4096]{1,0:T(8,128)(2,1)} %q_hbm.1, bf16[32,4096]{1,0:T(8,128)(2,1)} %k_hbm.1, bf16[32,4096]{1,0:T(8,128)(2,1)} %v_hbm.1, bf16[32,5120]{1,0:T(8,128)(2,1)} %hid_hbm.1, bf16[256,5120]{1,0:T(8,128)(2,1)} %wo_hbm.1, ...), custom_call_target="tpu_custom_call" | custom-call | tf_op jit(solution)/shard_map/pallas_call | solution.py:632
  116.0 1.0 shard_map.185

commit v6 on v5

--- a/solution.py
+++ b/solution.py
@@ -367,7 +367,7 @@
                 dst_ref=ref,
                 send_sem=low_send.at[self.t],
                 recv_sem=low_recv.at[self.t],
-                device_id={"mlp": lax.rem(m + i, 16)},
+                device_id={"mlp": up1(y, far_first(lax.div(i, 4))) * 4 + up1(z, far_first(lax.rem(i, 4)))},
                 device_id_type=MESH,
             )
 
@@ -388,7 +388,7 @@
                 self.low_copy(i).start()
                 return c
 
-            lax.fori_loop(1, 16, low_start, 0)
+            lax.fori_loop(0, 15, low_start, 0)
 
         def activate(self):
             t, rows = self.t, rows_of(self.t)

time: 117 us -> 118 us (level)
  no operation moved by 1% of the time
where the time goes in v6:
time: 118 us
  Pallas kernels  117 us (99%)
    pallas_call x1, Pallas kernels, shards(): pl.pallas_call(kernel, out_shape=(pltpu.VMEM((32, WIDTH), BF16), pltpu.VM...  116 us

profile of v6, /device:TPU:0, one launch (start us, length us, event | category | flops | bytes accessed | tf_op | source)
XLA Modules:
  0.0 117.6 jit_solution(8237003562036376292)
XLA Ops:
  0.6 115.8 %shard_map.184 = (bf16[32,5120]{1,0:T(8,128)(2,1)S(1)}, bf16[5,128,256]{2,1,0:T(8,128)(2,1)S(1)}, bf16[5,128,256]{2,1,0:T(8,128)(2,1)S(1)}) custom-call(bf16[32,4096]{1,0:T(8,128)(2,1)} %q_hbm.1, bf16[32,4096]{1,0:T(8,128)(2,1)} %k_hbm.1, bf16[32,4096]{1,0:T(8,128)(2,1)} %v_hbm.1, bf16[32,5120]{1,0:T(8,128)(2,1)} %hid_hbm.1, bf16[256,5120]{1,0:T(8,128)(2,1)} %wo_hbm.1, ...), custom_call_target="tpu_custom_call" | custom-call | tf_op jit(solution)/shard_map/pallas_call | solution.py:632
  116.4 1.0 shard_map.185
